TPU v7x, 32 devices: a whole 2x2x4 slice. The times are simulated.
32 devices in a mesh: gx: 2 (over core), gy: 4 (over y, x), gz: 4 (over z).
Axes of the slice: x: 2, y: 2, z: 4, core: 2. Of those that a mesh axis runs over, the one named last changes fastest.
Arguments:
- jacobian: bfloat16 [1024, 7, 135, 135], P(('gx', 'gy', 'gz')), may hold values from -6 to 6
- prolong: bfloat16 [1024, 135, 135], P(('gx', 'gy', 'gz')), may hold values from -0.5 to 0.5
- residual: bfloat16 [1024, 135], P(('gx', 'gy', 'gz')), may hold values from -6 to 6
- neighbours: int32 [1024, 6], P(('gx', 'gy', 'gz')), may hold values from -1 to 1023, as said below
- agg_map: int32 [1024], P(('gx', 'gy', 'gz')), may hold values from 0 to 127, as said below
- owners: int32 [128], P(('gx', 'gy', 'gz')), may hold values from 0 to 3, as said below
Outputs:
- coarse: bfloat16 [128, 7, 135, 135], P(('gx', 'gy', 'gz'))
- restricted: bfloat16 [128, 135], P(('gx', 'gy', 'gz'))
Inputs may be any that keep to these rules, and one draw needn't show every extreme that they name: `neighbours`: elements form a structured grid of bricks of 4 x 4 x 2 per device, laid out by the device's gx, gy, gz index; inside a device their numbering is an arbitrary permutation. The neighbour in direction -x or +x lies on the same device or on the device one step along gx (likewise y with gy, z with gz); exactly 8, 8 and 16 elements of a device have their x, y and z neighbour of one side off the device or absent. `agg_map`: aggregates are cubes of 2 x 2 x 2 elements of one device's brick; device d holds aggregates d * 4 to (d + 1) * 4 - 1. `owners`: owners are multiples of 1; each device hands exactly 1 of its aggregates to each such owner.
All inputs are finite; a program needn't handle non-finite values.
Results may differ from a plain program's by a relative error of at most 0.0051.
Values may be sent and summed in bfloat16 or wider, within the bound.
A program may use at most 192 MiB of HBM per device.

v0:
```python
import jax
import jax.numpy as jnp
from jax import lax
from jax.experimental import pallas as pl
from jax.experimental.pallas import tpu as pltpu
from jax.sharding import PartitionSpec as P

LX = 4
LY = 4
LZ = 2
GROUPS = 4
LANES = 128
CHUNK = 4
MESH = pl.DeviceIdType.MESH


def mul(a, b):
    return jnp.dot(a, b, preferred_element_type=jnp.float32)


def lane_ids(shape):
    return lax.broadcasted_iota(jnp.int32, shape, 1)


def channels_of(size_x):
    z = [("gz", 1, LX * LY, 5), ("gz", -1, LX * LY, 4)]
    y = [("gy", 1, LX * LZ, 3), ("gy", -1, LX * LZ, 2)]
    if size_x == 2:
        x = [("gx", 0, LY * LZ, None)]
    else:
        x = [("gx", 1, LY * LZ, 1), ("gx", -1, LY * LZ, 0)]
    return z + y + x


def channel_offsets(channels, elems):
    offsets, at = [], elems
    for _, _, count, _ in channels:
        offsets.append(at)
        at += count
    return offsets, at


def face_rows(count, tall):
    return count * LANES + count * 8 + tall


def partner_bits(me, r):
    high, low = me // 2, me % 2
    high = high + (1 - r // 2) * (1 - 2 * high)
    low = low + (1 - r % 2) * (1 - 2 * low)
    return high * 2 + low


def fused_kernel(table, prolong, jac, residual, sizes, aggs_here):
    width, elems, _ = prolong.shape
    sides = jac.shape[0]
    size_x, size_y, size_z = sizes
    rest = width - LANES
    tall = pl.cdiv(width + 1, 8) * 8
    full = pl.cdiv(width + 1, 16) * 16
    pitch = elems + 1
    per_owner = aggs_here // GROUPS
    stride_z = size_z // GROUPS
    out_slots = size_z * per_owner
    members = elems // aggs_here
    on_face = members // 2
    channels = channels_of(size_x)
    offsets, zero_block = channel_offsets(channels, elems)
    nch = len(channels)
    tail = sides * LANES
    msg_rows = tail + LANES
    half = LANES // 2
    most = max(count for _, _, count, _ in channels)
    pieces = sides + 1
    step_rows = 5 if width % 5 == 0 else 1

    def kernel(table_ref, p_hbm, j_hbm, res_ref, rows_ref, *refs):
        praw, jraw, near, far, pool, pt, jm = refs[:7]
        sends, recvs = refs[7 : 7 + nch], refs[7 + nch : 7 + 2 * nch]
        remf, farf, msg, msg_rem, msg_far, racc, acc = refs[7 + 2 * nch : 14 + 2 * nch]
        p_sem, j_sem, f_send, f_recv, r_send, r_recv, self_sem = refs[14 + 2 * nch :]
        me = {"gx": lax.axis_index("gx"), "gy": lax.axis_index("gy"), "gz": lax.axis_index("gz")}
        size = {"gx": size_x, "gy": size_y, "gz": size_z}
        me_z = me["gz"]

        p_copy = pltpu.make_async_copy(p_hbm, praw, p_sem)
        p_copy.start()

        def j_copy(k):
            return pltpu.make_async_copy(j_hbm.at[k], jraw.at[k], j_sem.at[k])

        for k in range(sides):
            j_copy(k).start()

        barrier = pltpu.get_barrier_semaphore()
        for step in range(1, size_z):
            to = lax.rem(me_z + step, size_z)
            pl.semaphore_signal(barrier, inc=1, device_id={"gz": to}, device_id_type=MESH)
        expected = size_z - 1
        if size_x == 2:
            pl.semaphore_signal(
                barrier, inc=1, device_id={"gx": 1 - me["gx"]}, device_id_type=MESH
            )
            expected = expected + 1
        for axis in ["gy"] + (["gx"] if size_x > 2 else []):
            for step in (1, -1):
                there = me[axis] + step
                exists = (there >= 0) & (there < size[axis])

                @pl.when(exists)
                def _(axis=axis, there=there):
                    pl.semaphore_signal(
                        barrier, inc=1, device_id={axis: there}, device_id_type=MESH
                    )

                expected = expected + exists.astype(jnp.int32)

        msg_far[...] = jnp.zeros_like(msg_far)
        pool[zero_block] = jnp.zeros(pool.shape[1:], pool.dtype)

        def spread(load, last):
            @pl.loop(0, width // step_rows)
            def _(c):
                part = load(c).astype(jnp.float32)
                for i in range(step_rows):
                    rows = pl.ds((c * step_rows + i) * pitch, elems)
                    near[rows, :] = part[i, :, :LANES]
                    far[rows, :rest] = part[i, :, LANES:]

            near[pl.ds(width * pitch, elems), :] = last[:, :LANES]
            far[pl.ds(width * pitch, elems), :rest] = last[:, LANES:]

        def block(e):
            rows = pl.ds(e, width + 1, stride=pitch)
            right = far[rows, :]
            right = jnp.where(lane_ids(right.shape) < rest, right, 0.0)
            both = jnp.concatenate([near[rows, :], right], axis=1)[:, :full]
            below = jnp.zeros((full - width - 1, full), jnp.float32)
            return jnp.concatenate([both, below], axis=0)

        p_copy.wait()
        spread(
            lambda c: praw[pl.ds(c * step_rows, step_rows)],
            jnp.zeros((elems, width), jnp.float32),
        )

        @pl.loop(0, elems // 4)
        def _(group):
            for u in range(4):
                e = group * 4 + u
                whole = block(e)
                pool[e] = whole[:, :width].astype(pool.dtype)
                pt[e] = whole.T[:tall].astype(pt.dtype)

        pl.semaphore_wait(barrier, expected)

        def face_target(c):
            axis, step, _, _ = channels[c]
            return {axis: 1 - me[axis] if step == 0 else me[axis] + step}

        def when_sent(c):
            axis, step, _, _ = channels[c]
            if step == 0:
                return lambda f: f()
            there = me[axis] + step
            return pl.when((there >= 0) & (there < size[axis]))

        def when_received(c):
            axis, step, _, _ = channels[c]
            if step == 0:
                return lambda f: f()
            there = me[axis] - step
            return pl.when((there >= 0) & (there < size[axis]))

        def face_parts(c):
            count = channels[c][2]
            parts = [(n * LANES, CHUNK * LANES) for n in range(0, count, CHUNK)]
            return parts + [(count * LANES, count * 8 + full)]

        def face_copy(c, part):
            start, rows = face_parts(c)[part]
            return pltpu.make_async_remote_copy(
                src_ref=sends[c].at[pl.ds(start, rows)],
                dst_ref=recvs[c].at[pl.ds(start, rows)],
                send_sem=f_send.at[c, part],
                recv_sem=f_recv.at[c, part],
                device_id=face_target(c),
                device_id_type=MESH,
            )

        def pack(c, n):
            whole = pool[table_ref[c, n]]
            sends[c][n * LANES : (n + 1) * LANES, :] = whole[:LANES, :LANES]
            remf[c, n * 8 : (n + 1) * 8, :] = whole[LANES:tall, :LANES].astype(jnp.float32)
            farf[c, :, n * rest : (n + 1) * rest] = whole[:, LANES:width].astype(jnp.float32)

        def pack_tail(c):
            count = channels[c][2]
            at = count * LANES
            sends[c][at : at + count * 8, :] = remf[c, : count * 8, :].astype(jnp.bfloat16)
            sends[c][at + count * 8 : at + count * 8 + full, :] = farf[c].astype(jnp.bfloat16)

        def send_faces(group):
            parts = max(len(face_parts(c)) for c in group)
            for part in range(parts):
                for c in group:
                    if part < len(face_parts(c)):
                        if part < len(face_parts(c)) - 1:
                            for n in range(part * CHUNK, (part + 1) * CHUNK):
                                pack(c, n)
                        else:
                            pack_tail(c)

                        @when_sent(c)
                        def _(c=c, part=part):
                            face_copy(c, part).start()

        def take_faces(group):
            for c in group:

                @when_received(c)
                def _(c=c):
                    for part in range(len(face_parts(c))):
                        face_copy(c, part).wait_recv()
                    count = channels[c][2]
                    at = count * LANES
                    remf[c, : count * 8, :] = recvs[c][at : at + count * 8, :].astype(jnp.float32)
                    farf[c] = recvs[c][at + count * 8 : at + count * 8 + full, :].astype(
                        jnp.float32
                    )
                    for n in range(count):
                        to = offsets[c] + n
                        pool[to, :LANES, :LANES] = recvs[c][n * LANES : (n + 1) * LANES, :]
                        below = remf[c, n * 8 : (n + 1) * 8, :]
                        below = jnp.concatenate([below, jnp.zeros_like(below)], axis=0)
                        pool[to, LANES:full, :LANES] = below.astype(pool.dtype)
                        pool[to, :, LANES:width] = farf[
                            c, :, n * rest : (n + 1) * rest
                        ].astype(pool.dtype)

        send_faces([0, 1])
        send_faces(list(range(2, nch)))

        @pl.loop(0, sides)
        def _(k):
            j_copy(k).wait()
            own = (k == 0).astype(jnp.float32)
            spread(
                lambda c: jraw[k, pl.ds(c * step_rows, step_rows)],
                res_ref[...].astype(jnp.float32) * own,
            )

            @pl.loop(0, elems // 4)
            def _(group):
                for u in range(4):
                    e = group * 4 + u
                    jm[k, e] = block(e).astype(jm.dtype)

        my_group = me_z // stride_z

        def target_of(r):
            return partner_bits(my_group, r // per_owner) * stride_z

        def slot_of(z, r):
            return z * per_owner + r % per_owner

        def row_copy(r, piece):
            at = pl.ds(pl.multiple_of(piece * LANES, LANES), LANES)
            slot = slot_of(me_z, r)
            return pltpu.make_async_remote_copy(
                src_ref=msg.at[r, at],
                dst_ref=rows_ref.at[slot, at],
                send_sem=r_send.at[r, piece],
                recv_sem=r_recv.at[slot, piece],
                device_id={"gz": target_of(r)},
                device_id_type=MESH,
            )

        def send_row(r, piece):
            @pl.when(target_of(r) != me_z)
            def _():
                row_copy(r, piece).start()

        def emit(r, s, value):
            msg[r, s * LANES : (s + 1) * LANES, :] = value[:LANES, :LANES].astype(msg.dtype)
            msg_rem[r, s * 8 : (s + 1) * 8, :] = value[LANES:tall, :LANES]
            msg_far[r, :, s * rest : (s + 1) * rest] = value[:, LANES:width]
            send_row(r, s)

        def side_sum(r, d):
            total = None
            for m in range(on_face):
                code = table_ref[nch + 1 + d, r * on_face + m]
                e, n = code % elems, code // elems
                product = mul(jm[1 + d, e], pool[n]).astype(jnp.bfloat16)
                triple = mul(pt[e], product)
                total = triple if total is None else total + triple
            return total

        @pl.loop(0, aggs_here)
        def _(r):
            acc[...] = jnp.zeros_like(acc)
            racc[...] = jnp.zeros_like(racc)

            @pl.loop(0, members // 2)
            def _(pair):
                total = None
                for u in range(2):
                    code = table_ref[nch, r * members + pair * 2 + u]
                    e, code = code % elems, code // elems
                    product = mul(jm[0, e], pool[e])
                    for axis in range(3):
                        x, code = code % (2 * elems), code // (2 * elems)
                        k = 1 + 2 * axis + x // elems
                        product = product + mul(jm[k, e], pool[x % elems])
                    racc[...] += product[LANES:tall]
                    triple = mul(pt[e], product.astype(jnp.bfloat16))
                    total = triple if total is None else total + triple
                acc[...] += total

            below = racc[...]
            spare = lax.broadcasted_iota(jnp.int32, below.shape, 0) == width - LANES
            acc[LANES:tall, :] += jnp.where(spare, below, 0.0)
            emit(r, 0, acc[...])

        take_faces(list(range(2, nch)))

        @pl.loop(0, aggs_here)
        def _(r):
            for d in range(sides - 3):
                emit(r, 1 + d, side_sum(r, d))

        take_faces([0, 1])

        @pl.loop(0, aggs_here)
        def _(r):
            for d in range(sides - 3, sides - 1):
                emit(r, 1 + d, side_sum(r, d))
            msg_rem[r, sides * 8 : (sides + 1) * 8, :] = msg_far[r, LANES:tall, :]
            msg[r, tail : tail + half, :] = msg_rem[r].astype(msg.dtype)
            right = pltpu.roll(msg_far[r, half:LANES, :], half, 1)
            left = msg_far[r, :half, :]
            folded = jnp.where(lane_ids(left.shape) < half, left, right)
            msg[r, tail + half : msg_rows, :] = folded.astype(msg.dtype)
            send_row(r, sides)

        def self_copy(r):
            return pltpu.make_async_copy(
                msg.at[r], rows_ref.at[slot_of(me_z, r)], self_sem.at[r % per_owner]
            )

        for sub in range(per_owner):
            r = aggs_here - per_owner + sub

            @pl.when(target_of(r) == me_z)
            def _(r=r):
                self_copy(r).start()

        for c in range(nch):

            @when_sent(c)
            def _(c=c):
                for part in range(len(face_parts(c))):
                    face_copy(c, part).wait_send()

        @pl.loop(0, aggs_here)
        def _(r):
            @pl.when(target_of(r) != me_z)
            def _():
                for piece in range(pieces):
                    row_copy(r, piece).wait_send()

        def row_arrival(slot, piece):
            at = pl.ds(piece * LANES, LANES)
            return pltpu.make_async_remote_copy(
                src_ref=msg.at[0, at],
                dst_ref=rows_ref.at[slot, at],
                send_sem=r_send.at[0, piece],
                recv_sem=r_recv.at[slot, piece],
                device_id={"gz": me_z},
                device_id_type=MESH,
            )

        owner = me_z % stride_z == 0

        @pl.when(owner)
        def _():
            @pl.loop(0, out_slots)
            def _(slot):
                @pl.when(slot // per_owner != me_z)
                def _():
                    for piece in range(pieces):
                        row_arrival(slot, piece).wait_recv()

        if stride_z > 1:

            @pl.when(jnp.logical_not(owner))
            def _():
                rows_ref[...] = jnp.zeros_like(rows_ref)

        for sub in range(per_owner):
            r = aggs_here - per_owner + sub

            @pl.when(target_of(r) == me_z)
            def _(r=r):
                self_copy(r).wait()

    bf16, f32 = jnp.bfloat16, jnp.float32
    spread_rows = (width + 1) * pitch
    faces = [pltpu.VMEM((face_rows(count, full), LANES), bf16) for _, _, count, _ in channels]
    parts = most // CHUNK + 1
    scratch = [
        pltpu.VMEM((width, elems, width), bf16),
        pltpu.VMEM((sides, width, elems, width), bf16),
        pltpu.VMEM((spread_rows, LANES), f32),
        pltpu.VMEM((spread_rows, LANES), f32),
        pltpu.VMEM((zero_block + 1, full, width), bf16),
        pltpu.VMEM((elems, tall, full), bf16),
        pltpu.VMEM((sides, elems, full, full), bf16),
        *faces,
        *faces,
        pltpu.VMEM((nch, most * 8, LANES), f32),
        pltpu.VMEM((nch, full, LANES), f32),
        pltpu.VMEM((aggs_here, msg_rows, LANES), bf16),
        pltpu.VMEM((aggs_here, (sides + 1) * 8, LANES), f32),
        pltpu.VMEM((aggs_here, tall, LANES), f32),
        pltpu.VMEM((8, width), f32),
        pltpu.VMEM((tall, width), f32),
        pltpu.SemaphoreType.DMA,
        pltpu.SemaphoreType.DMA((sides,)),
        pltpu.SemaphoreType.DMA((nch, parts)),
        pltpu.SemaphoreType.DMA((nch, parts)),
        pltpu.SemaphoreType.DMA((aggs_here, pieces)),
        pltpu.SemaphoreType.DMA((out_slots, pieces)),
        pltpu.SemaphoreType.DMA((per_owner,)),
    ]
    return pl.pallas_call(
        kernel,
        in_specs=[
            pl.BlockSpec(memory_space=pltpu.SMEM),
            pl.BlockSpec(memory_space=pl.ANY),
            pl.BlockSpec(memory_space=pl.ANY),
            pl.BlockSpec(memory_space=pltpu.VMEM),
        ],
        out_specs=pl.BlockSpec(memory_space=pltpu.VMEM),
        out_shape=jax.ShapeDtypeStruct((out_slots, msg_rows, LANES), bf16),
        scratch_shapes=scratch,
        compiler_params=pltpu.CompilerParams(
            collective_id=0, has_side_effects=True, vmem_limit_bytes=62 << 20
        ),
    )(table, prolong, jac, residual)


def tables(neighbours, agg_map, owners, device, elems, sizes):
    size_x, _, size_z = sizes
    aggs_here = owners.shape[0]
    per_owner = aggs_here // GROUPS
    stride_z = size_z // GROUPS
    members = elems // aggs_here
    on_face = members // 2
    channels = channels_of(size_x)
    offsets, zero_block = channel_offsets(channels, elems)
    most = max(count for _, _, count, _ in channels)
    nbr = neighbours.T
    local = nbr - device * elems
    here = (local >= 0) & (local < elems)
    valid = nbr >= 0
    ids = jnp.arange(elems, dtype=jnp.int32)
    agg = agg_map - device * aggs_here
    before = ids[None, :] < ids[:, None]

    away = jnp.logical_not(here)
    rank = jnp.sum((away[:, None, :] & before[None]).astype(jnp.int32), axis=2)
    places = jnp.arange(most, dtype=jnp.int32)
    chosen = away[:, None, :] & (rank[:, None, :] == places[None, :, None])
    by_side = jnp.sum(jnp.where(chosen, ids, 0), axis=2)

    away_valid = away & valid
    lower = away_valid[:, None, :] & (nbr[:, None, :] < nbr[:, :, None])
    position = jnp.sum(lower.astype(jnp.int32), axis=2)
    x_from = [4, 4] if size_x == 2 else [4, 5]
    source = jnp.array([offsets[c] for c in x_from + [2, 3, 0, 1]], jnp.int32)[:, None]
    index = jnp.where(here, local, source + position)
    index = jnp.where(valid, index, zero_block)
    near_agg = jnp.sum(jnp.where(local[:, :, None] == ids, agg, 0), axis=2)
    same = here & (near_agg == agg[None, :])

    count = jnp.arange(aggs_here, dtype=jnp.int32)
    earlier = (owners[None, :] == owners[:, None]) & (count[None, :] < count[:, None])
    within = jnp.sum(earlier.astype(jnp.int32), axis=1)
    mine = lax.axis_index("gz") // stride_z
    to = owners // stride_z
    turn = 3 - (2 * jnp.abs(to // 2 - mine // 2) + jnp.abs(to % 2 - mine % 2))
    order = turn * per_owner + within
    order_e = jnp.sum(jnp.where(agg[:, None] == count, order, 0), axis=1)

    together = before & (order_e[None, :] == order_e[:, None])
    m_place = order_e * members + jnp.sum(together.astype(jnp.int32), axis=1)
    inner = [
        jnp.where(same[2 * a + 1], elems + local[2 * a + 1], local[2 * a]) for a in range(3)
    ]
    wide = 2 * elems
    m_code = ids + elems * (inner[0] + wide * (inner[1] + wide * inner[2]))
    m_row = jnp.sum(jnp.where(m_place[None, :] == ids[:, None], m_code, 0), axis=1)

    outer = jnp.logical_not(same)
    s_rank = jnp.sum((outer[:, None, :] & together[None]).astype(jnp.int32), axis=2)
    s_place = jnp.where(outer, order_e * on_face + s_rank, -1)
    slots = jnp.arange(aggs_here * on_face, dtype=jnp.int32)
    s_code = ids + elems * index
    s_hit = s_place[:, None, :] == slots[None, :, None]
    s_rows = jnp.sum(jnp.where(s_hit, s_code[:, None, :], 0), axis=2)

    if size_x == 2:
        swap = jnp.where(lax.axis_index("gx") == 0, by_side[1], by_side[0])
        picks = jnp.stack([by_side[5], by_side[4], by_side[3], by_side[2], swap])
    else:
        picks = by_side[::-1][jnp.array([0, 1, 2, 3, 4, 5])]

    def padded(rows):
        return jnp.pad(rows, ((0, 0), (0, elems - rows.shape[1])))

    return jnp.concatenate([padded(picks), m_row[None], padded(s_rows)], axis=0)


def body(jacobian, prolong, residual, neighbours, agg_map, owners):
    elems = jacobian.shape[0]
    sides = jacobian.shape[1]
    width = prolong.shape[1]
    aggs_here = owners.shape[0]
    rest = width - LANES
    half = LANES // 2
    sizes = tuple(lax.axis_size(a) for a in ("gx", "gy", "gz"))
    place = tuple(lax.axis_index(a) for a in ("gx", "gy", "gz"))
    device = (place[0] * sizes[1] + place[1]) * sizes[2] + place[2]
    table = tables(neighbours, agg_map, owners, device, elems, sizes)
    jac = jnp.transpose(jacobian, (1, 2, 0, 3))
    pro = jnp.transpose(prolong, (1, 0, 2))
    rows = fused_kernel(table, pro, jac, residual, sizes, aggs_here)

    tail = sides * LANES
    slots = rows.shape[0]
    head = rows[:, :tail].reshape(slots, sides, LANES, LANES)
    below = rows[:, tail : tail + sides * 8].reshape(slots, sides, 8, LANES)
    last = rows[:, tail + sides * 8 : tail + half]
    folded = rows[:, tail + half :]
    used = sides * rest
    far = jnp.concatenate(
        [folded[:, :, :used], folded[:, :, half : half + used], last[:, :rest, :used]], axis=1
    )
    far = far.reshape(slots, width, sides, rest).transpose(0, 2, 1, 3)
    heads = jnp.concatenate([head, below[:, :, :rest]], axis=2)
    coarse = jnp.concatenate([heads, far], axis=3)
    restricted = jnp.concatenate([below[:, 0, rest], last[:, rest, :rest]], axis=1)
    return coarse, restricted


def solution(mesh):
    spec = P(("gx", "gy", "gz"))
    return jax.shard_map(
        body,
        mesh=mesh,
        in_specs=(spec,) * 6,
        out_specs=(spec, spec),
        check_vma=False,
    )
```

profile of v0, /device:TPU:0, one launch (start us, length us, event | category | flops | bytes accessed | tf_op | source)
XLA Modules:
  0.0 70.7 jit_solution(7549354934854868264)
XLA Ops:
  0.7 0.7 broadcast_subtract_fusion.1
  1.3 0.9 %convert_reduce_fusion.4 = s32[4]{0:T(128)S(1)} fusion(s32[4]{0:T(128)} %param.12), kind=kLoop, calls=%fused_computation.26 | loop fusion | flops 76 | bytes 32 | tf_op jit(solution)/shard_map/reduce_sum | solution.py:490
  2.2 0.7 subtract_add_fusion
  2.9 0.1 select_reduce_fusion.4
  3.0 0.2 convert_reduce_fusion.3
  3.2 0.1 compare_and_fusion
  3.3 0.7 fusion.8
  4.0 0.4 select_reduce_fusion
  4.3 0.7 fusion.9
  5.0 0.2 convert_reduce_fusion.1
  5.2 0.1 select_reduce_fusion.3
  5.4 0.2 select_reduce_fusion.2
  5.6 1.0 %convert_reduce_fusion = s32[6,32]{1,0:T(8,128)S(1)} fusion(s32[6,32]{1,0:T(8,128)} %bitcast.28, pred[6,32]{1,0:T(8,128)(4,1)S(1)} %get-tuple-element.16), kind=kLoop, calls=%fused_computation.2 | loop fusion | flops 24384 | bytes 1728 | tf_op jit(solution)/shard_map/reduce_sum | solution.py:480
  6.6 0.7 %multiply_add_fusion = s32[6,32]{1,0:T(8,128)S(1)} fusion(pred[6,32]{1,0:T(8,128)(4,1)S(1)} %get-tuple-element.17, pred[6,32]{1,0:T(8,128)(4,1)S(1)} %get-tuple-element.3, s32[6,32]{1,0:T(8,128)S(1)} %get-tuple-element.4, s32[6,32]{1,0:T(8,128)S(1)} %convert_reduce_fusion, s32[6]{0:T(128)} %constant.91.clone), kind=kLoop, calls=%fused_computation.20 | loop fusion | flops 960 | bytes 2712 | tf_op jit(solution)/shard_map/add | solution.py:510
  7.3 0.2 select_reduce_fusion.1
  7.5 0.6 pad_add_fusion.table_ref
  8.1 52.1 %shard_map.86 = bf16[4,1024,128]{2,1,0:T(8,128)(2,1)} custom-call(s32[12,32]{1,0:T(8,128)} %pad_add_fusion.table_ref, bf16[135,32,135]{2,1,0:T(8,128)(2,1)} %bitcast.25, bf16[7,135,32,135]{3,2,1,0:T(8,128)(2,1)} %bitcast.23, bf16[32,135]{1,0:T(8,128)(2,1)} %res_ref.1), custom_call_target="tpu_custom_call" | custom-call | tf_op jit(solution)/shard_map/pallas_call | solution.py:437
  60.3 0.7 slice.97
  61.0 0.7 slice.95
  61.7 0.8 %slice_bitcast_fusion = bf16[4,7,8,128]{3,2,1,0:T(8,128)(2,1)S(1)} fusion(bf16[4,1024,128]{2,1,0:T(8,128)(2,1)} %shard_map.86), kind=kLoop, calls=%fused_computation.7 | loop fusion | bytes 114688 | tf_op jit(solution)/shard_map/reshape | solution.py:544
  62.5 0.6 pad_maximum_fusion.2
  63.1 1.0 %fusion.10 = (bf16[4,64,49]{2,1,0:T(8,128)(2,1)S(1)}, bf16[4,64,49]{2,1,0:T(8,128)(2,1)S(1)}) fusion(bf16[4,1024,128]{2,1,0:T(8,128)(2,1)} %shard_map.86), kind=kLoop, calls=%fused_computation.57 | loop fusion | bytes 100352 | tf_op jit(solution)/shard_map/slice | solution.py:549
  64.2 1.2 %slice.90 = bf16[4,896,128]{2,1,0:T(8,128)(2,1)S(1)} slice(bf16[4,1024,128]{2,1,0:T(8,128)(2,1)} %shard_map.86), slice={[0:4], [0:896], [0:128]} | slice | bytes 1835008 | tf_op jit(solution)/shard_map/slice | solution.py:543
  65.4 0.7 %copy.19 = bf16[4,7,128,128]{3,0,2,1:T(4,128)(2,1)S(1)} copy(bf16[4,7,128,128]{3,2,1,0:T(8,128)(2,1)S(1)} %bitcast.24) | data formatting | bytes 1835008 | tf_op jit(solution)/shard_map/reshape | solution.py:543
  66.2 0.2 copy.20
  66.3 1.8 %copy.21 = bf16[4,7,135,7]{3,0,2,1:T(4,128)(2,1)S(1)} copy(bf16[4,7,135,7]{2,0,3,1:T(4,128)(2,1)S(1)} %bitcast.26) | data formatting | bytes 105840 | tf_op jit(solution)/shard_map/transpose | solution.py:551
  68.2 2.6 %pad_maximum_fusion = bf16[4,7,135,135]{3,0,2,1:T(4,128)(2,1)} fusion(bf16[4,7,135,7]{3,0,2,1:T(4,128)(2,1)S(1)} %copy.21, bf16[4,7,7,128]{3,0,2,1:T(4,128)(2,1)S(1)} %copy.24, bf16[4,7,128,128]{3,0,2,1:T(4,128)(2,1)S(1)} %copy.19), kind=kLoop, calls=%fused_computation | loop fusion | flops 3061800 | bytes 2041200 | tf_op jit(solution)/shard_map/concatenate | solution.py:553
  (11 shorter events, 0.1 us)
where the time goes:
time: 71.3 us; the launch traced here: 70.7 us
  Pallas kernels  52.1 us (73%)
  other arithmetic  10.6 us (15%)
  local copies, waits for them, and re-layouts  7.24 us (10%)
  between operations  0.76 us (1%)
    pallas_call x1, Pallas kernels, fused_kernel(): pl.pallas_call(kernel, in_specs=[pl.BlockSpec(memory_space=pltpu.SMEM), p...  52.1 us
    concatenate x1, other arithmetic, body(): coarse = jnp.concatenate([heads, far], axis=3)  2.56 us
    transpose x1, local copies, waits for them, and re-layouts, body(): far = far.reshape(slots, width, sides, rest).transpose(0, 2, 1, 3)  1.82 us

commit v1 on v0

--- a/solution.py
+++ b/solution.py
@@ -11,6 +11,7 @@
 GROUPS = 4
 LANES = 128
 CHUNK = 4
+AHEAD = 4
 MESH = pl.DeviceIdType.MESH
 
 
@@ -51,9 +52,10 @@
     return high * 2 + low
 
 
-def fused_kernel(table, prolong, jac, residual, sizes, aggs_here):
+def fused_kernel(neighbours, agg_map, owners, prolong, jac, residual, sizes):
     width, elems, _ = prolong.shape
     sides = jac.shape[0]
+    aggs_here = owners.shape[1]
     size_x, size_y, size_z = sizes
     rest = width - LANES
     tall = pl.cdiv(width + 1, 8) * 8
@@ -72,13 +74,16 @@
     half = LANES // 2
     most = max(count for _, _, count, _ in channels)
     pieces = sides + 1
+    early = aggs_here // 2
     step_rows = 5 if width % 5 == 0 else 1
 
-    def kernel(table_ref, p_hbm, j_hbm, res_ref, rows_ref, *refs):
-        praw, jraw, near, far, pool, pt, jm = refs[:7]
-        sends, recvs = refs[7 : 7 + nch], refs[7 + nch : 7 + 2 * nch]
-        remf, farf, msg, msg_rem, msg_far, racc, acc = refs[7 + 2 * nch : 14 + 2 * nch]
-        p_sem, j_sem, f_send, f_recv, r_send, r_recv, self_sem = refs[14 + 2 * nch :]
+    def kernel(nbr_ref, agg_ref, own_ref, p_hbm, j_hbm, res_ref, out_ref, rest_ref, *refs):
+        tab, table_ref, praw, jraw, near, far, pool, pt, jm = refs[:9]
+        sends, recvs = refs[9 : 9 + nch], refs[9 + nch : 9 + 2 * nch]
+        refs = refs[9 + 2 * nch :]
+        remf, farf, msg, msg_rem, msg_far, racc, acc = refs[:7]
+        rows_ref, mixed, mixed_rem, mixed_rest = refs[7:11]
+        t_sem, p_sem, j_sem, f_send, f_recv, r_send, r_recv, self_sem = refs[11:]
         me = {"gx": lax.axis_index("gx"), "gy": lax.axis_index("gy"), "gz": lax.axis_index("gz")}
         size = {"gx": size_x, "gy": size_y, "gz": size_z}
         me_z = me["gz"]
@@ -87,10 +92,8 @@
         p_copy.start()
 
         def j_copy(k):
-            return pltpu.make_async_copy(j_hbm.at[k], jraw.at[k], j_sem.at[k])
-
-        for k in range(sides):
-            j_copy(k).start()
+            slot = k % AHEAD
+            return pltpu.make_async_copy(j_hbm.at[k], jraw.at[slot], j_sem.at[slot])
 
         barrier = pltpu.get_barrier_semaphore()
         for step in range(1, size_z):
@@ -138,7 +141,22 @@
             below = jnp.zeros((full - width - 1, full), jnp.float32)
             return jnp.concatenate([both, below], axis=0)
 
+        device = (me["gx"] * size_y + me["gy"]) * size_z + me_z
+        write_table(
+            tab,
+            nbr_ref[...],
+            agg_ref[...] - device * aggs_here,
+            own_ref[...],
+            device * elems,
+            me_z // stride_z,
+            me["gx"],
+            sizes,
+        )
+        t_copy = pltpu.make_async_copy(tab, table_ref, t_sem)
+        t_copy.start()
         p_copy.wait()
+        for k in range(AHEAD):
+            j_copy(k).start()
         spread(
             lambda c: praw[pl.ds(c * step_rows, step_rows)],
             jnp.zeros((elems, width), jnp.float32),
@@ -148,10 +166,9 @@
         def _(group):
             for u in range(4):
                 e = group * 4 + u
-                whole = block(e)
-                pool[e] = whole[:, :width].astype(pool.dtype)
-                pt[e] = whole.T[:tall].astype(pt.dtype)
-
+                pool[e] = block(e)[:, :width].astype(pool.dtype)
+
+        t_copy.wait()
         pl.semaphore_wait(barrier, expected)
 
         def face_target(c):
@@ -189,7 +206,7 @@
             )
 
         def pack(c, n):
-            whole = pool[table_ref[c, n]]
+            whole = pool[table_ref[c, n] % elems]
             sends[c][n * LANES : (n + 1) * LANES, :] = whole[:LANES, :LANES]
             remf[c, n * 8 : (n + 1) * 8, :] = whole[LANES:tall, :LANES].astype(jnp.float32)
             farf[c, :, n * rest : (n + 1) * rest] = whole[:, LANES:width].astype(jnp.float32)
@@ -241,14 +258,24 @@
         send_faces([0, 1])
         send_faces(list(range(2, nch)))
 
+        @pl.loop(0, elems // 4)
+        def _(group):
+            for u in range(4):
+                e = group * 4 + u
+                pt[e] = block(e).T[:tall].astype(pt.dtype)
+
         @pl.loop(0, sides)
         def _(k):
             j_copy(k).wait()
             own = (k == 0).astype(jnp.float32)
             spread(
-                lambda c: jraw[k, pl.ds(c * step_rows, step_rows)],
+                lambda c: jraw[k % AHEAD, pl.ds(c * step_rows, step_rows)],
                 res_ref[...].astype(jnp.float32) * own,
             )
+
+            @pl.when(k + AHEAD < sides)
+            def _():
+                j_copy(k + AHEAD).start()
 
             @pl.loop(0, elems // 4)
             def _(group):
@@ -276,10 +303,22 @@
                 device_id_type=MESH,
             )
 
+        def self_copy(r, piece):
+            at = pl.ds(pl.multiple_of(piece * LANES, LANES), LANES)
+            return pltpu.make_async_copy(
+                msg.at[r, at],
+                rows_ref.at[slot_of(me_z, r), at],
+                self_sem.at[r % per_owner, piece],
+            )
+
         def send_row(r, piece):
             @pl.when(target_of(r) != me_z)
             def _():
                 row_copy(r, piece).start()
+
+            @pl.when(target_of(r) == me_z)
+            def _():
+                self_copy(r, piece).start()
 
         def emit(r, s, value):
             msg[r, s * LANES : (s + 1) * LANES, :] = value[:LANES, :LANES].astype(msg.dtype)
@@ -291,14 +330,13 @@
             total = None
             for m in range(on_face):
                 code = table_ref[nch + 1 + d, r * on_face + m]
-                e, n = code % elems, code // elems
+                e, n = code % elems, jnp.clip(code // elems, 0, zero_block)
                 product = mul(jm[1 + d, e], pool[n]).astype(jnp.bfloat16)
                 triple = mul(pt[e], product)
                 total = triple if total is None else total + triple
             return total
 
-        @pl.loop(0, aggs_here)
-        def _(r):
+        def own_slot(r):
             acc[...] = jnp.zeros_like(acc)
             racc[...] = jnp.zeros_like(racc)
 
@@ -323,19 +361,7 @@
             acc[LANES:tall, :] += jnp.where(spare, below, 0.0)
             emit(r, 0, acc[...])
 
-        take_faces(list(range(2, nch)))
-
-        @pl.loop(0, aggs_here)
-        def _(r):
-            for d in range(sides - 3):
-                emit(r, 1 + d, side_sum(r, d))
-
-        take_faces([0, 1])
-
-        @pl.loop(0, aggs_here)
-        def _(r):
-            for d in range(sides - 3, sides - 1):
-                emit(r, 1 + d, side_sum(r, d))
+        def send_tail(r):
             msg_rem[r, sides * 8 : (sides + 1) * 8, :] = msg_far[r, LANES:tall, :]
             msg[r, tail : tail + half, :] = msg_rem[r].astype(msg.dtype)
             right = pltpu.roll(msg_far[r, half:LANES, :], half, 1)
@@ -344,31 +370,25 @@
             msg[r, tail + half : msg_rows, :] = folded.astype(msg.dtype)
             send_row(r, sides)
 
-        def self_copy(r):
-            return pltpu.make_async_copy(
-                msg.at[r], rows_ref.at[slot_of(me_z, r)], self_sem.at[r % per_owner]
-            )
-
-        for sub in range(per_owner):
-            r = aggs_here - per_owner + sub
-
-            @pl.when(target_of(r) == me_z)
-            def _(r=r):
-                self_copy(r).start()
-
-        for c in range(nch):
-
-            @when_sent(c)
-            def _(c=c):
-                for part in range(len(face_parts(c))):
-                    face_copy(c, part).wait_send()
-
-        @pl.loop(0, aggs_here)
-        def _(r):
-            @pl.when(target_of(r) != me_z)
-            def _():
-                for piece in range(pieces):
-                    row_copy(r, piece).wait_send()
+        @pl.loop(0, 2)
+        def _(part):
+            first, last = part * early, part * early + early
+            pl.loop(first, last)(own_slot)
+            axis_faces = [list(range(4, nch)), [2, 3], [0, 1]]
+            for axis in range(3):
+
+                @pl.when(part == 0)
+                def _(axis=axis):
+                    take_faces(axis_faces[axis])
+
+                @pl.loop(first, last)
+                def _(r, axis=axis):
+                    for d in (2 * axis, 2 * axis + 1):
+                        emit(r, 1 + d, side_sum(r, d))
+                    if axis == 2:
+                        send_tail(r)
+
+        owner = me_z % stride_z == 0
 
         def row_arrival(slot, piece):
             at = pl.ds(piece * LANES, LANES)
@@ -381,37 +401,87 @@
                 device_id_type=MESH,
             )
 
-        owner = me_z % stride_z == 0
-
-        @pl.when(owner)
-        def _():
-            @pl.loop(0, out_slots)
-            def _(slot):
-                @pl.when(slot // per_owner != me_z)
-                def _():
-                    for piece in range(pieces):
-                        row_arrival(slot, piece).wait_recv()
-
-        if stride_z > 1:
+        def arrive(piece):
+            for slot in range(out_slots):
+                mine = slot // per_owner == me_z
+
+                @pl.when(mine)
+                def _(slot=slot):
+                    self_copy(aggs_here - per_owner + slot % per_owner, piece).wait()
+
+                @pl.when(jnp.logical_not(mine))
+                def _(slot=slot):
+                    row_arrival(slot, piece).wait_recv()
+
+        def scatter(ref, slot, start, value):
+            count = value.shape[0]
+            ref[pl.ds(start * out_slots + slot, count, stride=out_slots), :] = value
+
+        def gathered(ref, count):
+            value = ref[: count * out_slots, :].astype(jnp.bfloat16)
+            return value.reshape(count, out_slots, LANES)
+
+        def unpack():
+            for s in range(sides):
+                arrive(s)
+                for slot in range(out_slots):
+                    block_of = rows_ref[slot, s * LANES : (s + 1) * LANES, :]
+                    scatter(mixed, slot, 0, block_of.astype(jnp.float32))
+                out_ref[s, :LANES, :, :LANES] = gathered(mixed, LANES)
+
+            arrive(sides)
+            for slot in range(out_slots):
+                below = rows_ref[slot, tail : tail + half, :].astype(jnp.float32)
+                folded = rows_ref[slot, tail + half : msg_rows, :].astype(jnp.float32)
+                scatter(mixed, slot, 0, folded)
+                scatter(mixed, slot, half, pltpu.roll(folded, half, 1))
+                scatter(mixed, slot, LANES, below[sides * 8 :])
+                for s in range(sides):
+                    scatter(mixed_rem.at[s], slot, 0, below[s * 8 : (s + 1) * 8])
+                mixed_rest[slot : slot + 1, :LANES] = below[rest : rest + 1]
+                at = sides * 8 + rest
+                mixed_rest[slot : slot + 1, LANES:] = below[at : at + 1, :rest]
+            rest_ref[...] = mixed_rest[:out_slots].astype(rest_ref.dtype)
+            right = gathered(mixed, tall)
+            for s in range(sides):
+                low = gathered(mixed_rem.at[s], 8)
+                out_ref[s, LANES:, :, :LANES] = low[:rest]
+                out_ref[s, :, :, LANES:] = right[:width, :, s * rest : (s + 1) * rest]
+
+        if stride_z == 1:
+            unpack()
+        else:
+            pl.when(owner)(unpack)
 
             @pl.when(jnp.logical_not(owner))
             def _():
-                rows_ref[...] = jnp.zeros_like(rows_ref)
-
-        for sub in range(per_owner):
-            r = aggs_here - per_owner + sub
-
-            @pl.when(target_of(r) == me_z)
-            def _(r=r):
-                self_copy(r).wait()
+                out_ref[...] = jnp.zeros_like(out_ref)
+                rest_ref[...] = jnp.zeros_like(rest_ref)
+
+        for c in range(nch):
+
+            @when_sent(c)
+            def _(c=c):
+                for part in range(len(face_parts(c))):
+                    face_copy(c, part).wait_send()
+
+        @pl.loop(0, aggs_here)
+        def _(r):
+            @pl.when(target_of(r) != me_z)
+            def _():
+                for piece in range(pieces):
+                    row_copy(r, piece).wait_send()
 
     bf16, f32 = jnp.bfloat16, jnp.float32
     spread_rows = (width + 1) * pitch
     faces = [pltpu.VMEM((face_rows(count, full), LANES), bf16) for _, _, count, _ in channels]
     parts = most // CHUNK + 1
+    table_rows = pl.cdiv(nch + sides, 8) * 8
     scratch = [
+        pltpu.VMEM((table_rows, LANES), jnp.int32),
+        pltpu.SMEM((table_rows, LANES), jnp.int32),
         pltpu.VMEM((width, elems, width), bf16),
-        pltpu.VMEM((sides, width, elems, width), bf16),
+        pltpu.VMEM((AHEAD, width, elems, width), bf16),
         pltpu.VMEM((spread_rows, LANES), f32),
         pltpu.VMEM((spread_rows, LANES), f32),
         pltpu.VMEM((zero_block + 1, full, width), bf16),
@@ -426,133 +496,143 @@
         pltpu.VMEM((aggs_here, tall, LANES), f32),
         pltpu.VMEM((8, width), f32),
         pltpu.VMEM((tall, width), f32),
+        pltpu.VMEM((out_slots, msg_rows, LANES), bf16),
+        pltpu.VMEM((tall * out_slots, LANES), f32),
+        pltpu.VMEM((sides, 8 * out_slots, LANES), f32),
+        pltpu.VMEM((pl.cdiv(out_slots, 8) * 8, width), f32),
         pltpu.SemaphoreType.DMA,
-        pltpu.SemaphoreType.DMA((sides,)),
+        pltpu.SemaphoreType.DMA,
+        pltpu.SemaphoreType.DMA((AHEAD,)),
         pltpu.SemaphoreType.DMA((nch, parts)),
         pltpu.SemaphoreType.DMA((nch, parts)),
         pltpu.SemaphoreType.DMA((aggs_here, pieces)),
         pltpu.SemaphoreType.DMA((out_slots, pieces)),
-        pltpu.SemaphoreType.DMA((per_owner,)),
+        pltpu.SemaphoreType.DMA((per_owner, pieces)),
     ]
     return pl.pallas_call(
         kernel,
-        in_specs=[
-            pl.BlockSpec(memory_space=pltpu.SMEM),
-            pl.BlockSpec(memory_space=pl.ANY),
-            pl.BlockSpec(memory_space=pl.ANY),
-            pl.BlockSpec(memory_space=pltpu.VMEM),
+        in_specs=[pl.BlockSpec(memory_space=pltpu.VMEM)] * 3
+        + [pl.BlockSpec(memory_space=pl.ANY)] * 2
+        + [pl.BlockSpec(memory_space=pltpu.VMEM)],
+        out_specs=[pl.BlockSpec(memory_space=pltpu.VMEM)] * 2,
+        out_shape=[
+            jax.ShapeDtypeStruct((sides, width, out_slots, width), bf16),
+            jax.ShapeDtypeStruct((out_slots, width), bf16),
         ],
-        out_specs=pl.BlockSpec(memory_space=pltpu.VMEM),
-        out_shape=jax.ShapeDtypeStruct((out_slots, msg_rows, LANES), bf16),
         scratch_shapes=scratch,
         compiler_params=pltpu.CompilerParams(
             collective_id=0, has_side_effects=True, vmem_limit_bytes=62 << 20
         ),
-    )(table, prolong, jac, residual)
-
-
-def tables(neighbours, agg_map, owners, device, elems, sizes):
+    )(neighbours, agg_map, owners, prolong, jac, residual)
+
+
+def write_table(tab, nbr, agg, owners, base, mine, x, sizes):
     size_x, _, size_z = sizes
-    aggs_here = owners.shape[0]
+    elems, aggs_here = nbr.shape[1], owners.shape[1]
     per_owner = aggs_here // GROUPS
     stride_z = size_z // GROUPS
     members = elems // aggs_here
     on_face = members // 2
     channels = channels_of(size_x)
     offsets, zero_block = channel_offsets(channels, elems)
-    most = max(count for _, _, count, _ in channels)
-    nbr = neighbours.T
-    local = nbr - device * elems
-    here = (local >= 0) & (local < elems)
-    valid = nbr >= 0
-    ids = jnp.arange(elems, dtype=jnp.int32)
-    agg = agg_map - device * aggs_here
-    before = ids[None, :] < ids[:, None]
-
-    away = jnp.logical_not(here)
-    rank = jnp.sum((away[:, None, :] & before[None]).astype(jnp.int32), axis=2)
-    places = jnp.arange(most, dtype=jnp.int32)
-    chosen = away[:, None, :] & (rank[:, None, :] == places[None, :, None])
-    by_side = jnp.sum(jnp.where(chosen, ids, 0), axis=2)
-
-    away_valid = away & valid
-    lower = away_valid[:, None, :] & (nbr[:, None, :] < nbr[:, :, None])
-    position = jnp.sum(lower.astype(jnp.int32), axis=2)
-    x_from = [4, 4] if size_x == 2 else [4, 5]
-    source = jnp.array([offsets[c] for c in x_from + [2, 3, 0, 1]], jnp.int32)[:, None]
-    index = jnp.where(here, local, source + position)
-    index = jnp.where(valid, index, zero_block)
-    near_agg = jnp.sum(jnp.where(local[:, :, None] == ids, agg, 0), axis=2)
-    same = here & (near_agg == agg[None, :])
-
-    count = jnp.arange(aggs_here, dtype=jnp.int32)
-    earlier = (owners[None, :] == owners[:, None]) & (count[None, :] < count[:, None])
-    within = jnp.sum(earlier.astype(jnp.int32), axis=1)
-    mine = lax.axis_index("gz") // stride_z
+    nch = len(channels)
+    square = (elems, elems)
+    down = lax.broadcasted_iota(jnp.int32, square, 0)
+    along = lax.broadcasted_iota(jnp.int32, square, 1)
+    ids = down[:, :1]
+
+    def flag(mask):
+        return jnp.where(mask, 1, 0)
+
+    eye = flag(down == along)
+    before = flag(along < down)
+
+    def by_row(value):
+        return jnp.sum(value, axis=1, keepdims=True)
+
+    def by_column(value):
+        return jnp.sum(value, axis=0, keepdims=True)
+
+    def column(row):
+        return by_row(eye * row)
+
+    def row(col):
+        return by_column(eye * col)
+
+    def listed(place, value):
+        return by_column(flag(place == along) * value)
+
+    def put(at, value):
+        tab[at : at + 1, :elems] = value
+
+    a_down = lax.broadcasted_iota(jnp.int32, (aggs_here, aggs_here), 0)
+    a_along = lax.broadcasted_iota(jnp.int32, (aggs_here, aggs_here), 1)
     to = owners // stride_z
     turn = 3 - (2 * jnp.abs(to // 2 - mine // 2) + jnp.abs(to % 2 - mine % 2))
-    order = turn * per_owner + within
-    order_e = jnp.sum(jnp.where(agg[:, None] == count, order, 0), axis=1)
-
-    together = before & (order_e[None, :] == order_e[:, None])
-    m_place = order_e * members + jnp.sum(together.astype(jnp.int32), axis=1)
-    inner = [
-        jnp.where(same[2 * a + 1], elems + local[2 * a + 1], local[2 * a]) for a in range(3)
-    ]
-    wide = 2 * elems
-    m_code = ids + elems * (inner[0] + wide * (inner[1] + wide * inner[2]))
-    m_row = jnp.sum(jnp.where(m_place[None, :] == ids[:, None], m_code, 0), axis=1)
-
-    outer = jnp.logical_not(same)
-    s_rank = jnp.sum((outer[:, None, :] & together[None]).astype(jnp.int32), axis=2)
-    s_place = jnp.where(outer, order_e * on_face + s_rank, -1)
-    slots = jnp.arange(aggs_here * on_face, dtype=jnp.int32)
-    s_code = ids + elems * index
-    s_hit = s_place[:, None, :] == slots[None, :, None]
-    s_rows = jnp.sum(jnp.where(s_hit, s_code[:, None, :], 0), axis=2)
+    turn = jnp.broadcast_to(turn, a_down.shape)
+    turn = by_row(jnp.where(a_down == a_along, turn, 0))
+    if per_owner > 1:
+        turn_row = by_column(jnp.where(a_down == a_along, turn, 0))
+        equal = flag(turn_row == turn) * flag(a_along < a_down)
+        turn = turn * per_owner + by_row(equal)
+    a_ids = lax.broadcasted_iota(jnp.int32, (aggs_here, elems), 0)
+    order_row = by_column(flag(agg == a_ids) * turn)
+    order = column(order_row)
+    agg_col = column(agg)
+    together = before * flag(order_row == order)
+    m_place = order * members + by_row(together)
 
     if size_x == 2:
-        swap = jnp.where(lax.axis_index("gx") == 0, by_side[1], by_side[0])
-        picks = jnp.stack([by_side[5], by_side[4], by_side[3], by_side[2], swap])
+        listing = [(5, 0), (4, 1), (3, 2), (2, 3)]
+        sources = [4, 4, 2, 3, 0, 1]
     else:
-        picks = by_side[::-1][jnp.array([0, 1, 2, 3, 4, 5])]
-
-    def padded(rows):
-        return jnp.pad(rows, ((0, 0), (0, elems - rows.shape[1])))
-
-    return jnp.concatenate([padded(picks), m_row[None], padded(s_rows)], axis=0)
+        listing = [(5, 0), (4, 1), (3, 2), (2, 3), (1, 4), (0, 5)]
+        sources = [4, 5, 2, 3, 0, 1]
+    sides_of, local_of, same_of = [], [], []
+    for d in range(6):
+        nbr_row = nbr[d : d + 1]
+        nbr_col = column(nbr_row)
+        local_row, local = nbr_row - base, nbr_col - base
+        away_row = 1 - flag(local_row >= 0) * flag(local_row < elems)
+        here = flag(local >= 0) * flag(local < elems)
+        rank = by_row(before * away_row)
+        place = jnp.where(here > 0, -1, rank)
+        sides_of.append(listed(place, ids))
+        crossing = away_row * flag(nbr_row >= 0)
+        position = by_row(crossing * flag(nbr_row < nbr_col))
+        index = jnp.where(here > 0, local, position + offsets[sources[d]])
+        index = jnp.where(nbr_col >= 0, index, zero_block)
+        near_agg = by_row(flag(local == along) * agg)
+        same = here * flag(near_agg == agg_col)
+        local_of.append(local)
+        same_of.append(same)
+        s_rank = by_row(together * (1 - row(same)))
+        s_place = jnp.where(same > 0, -1, order * on_face + s_rank)
+        put(nch + 1 + d, listed(s_place, ids + elems * index))
+    for d, c in listing:
+        put(c, sides_of[d])
+    if size_x == 2:
+        put(4, jnp.where(x == 0, sides_of[1], sides_of[0]))
+    code = jnp.zeros_like(ids)
+    for axis in (2, 1, 0):
+        after = same_of[2 * axis + 1] > 0
+        inner = jnp.where(after, local_of[2 * axis + 1] + elems, local_of[2 * axis])
+        code = code * (2 * elems) + inner
+    put(nch, listed(m_place, code * elems + ids))
 
 
 def body(jacobian, prolong, residual, neighbours, agg_map, owners):
-    elems = jacobian.shape[0]
-    sides = jacobian.shape[1]
-    width = prolong.shape[1]
-    aggs_here = owners.shape[0]
-    rest = width - LANES
-    half = LANES // 2
     sizes = tuple(lax.axis_size(a) for a in ("gx", "gy", "gz"))
-    place = tuple(lax.axis_index(a) for a in ("gx", "gy", "gz"))
-    device = (place[0] * sizes[1] + place[1]) * sizes[2] + place[2]
-    table = tables(neighbours, agg_map, owners, device, elems, sizes)
-    jac = jnp.transpose(jacobian, (1, 2, 0, 3))
-    pro = jnp.transpose(prolong, (1, 0, 2))
-    rows = fused_kernel(table, pro, jac, residual, sizes, aggs_here)
-
-    tail = sides * LANES
-    slots = rows.shape[0]
-    head = rows[:, :tail].reshape(slots, sides, LANES, LANES)
-    below = rows[:, tail : tail + sides * 8].reshape(slots, sides, 8, LANES)
-    last = rows[:, tail + sides * 8 : tail + half]
-    folded = rows[:, tail + half :]
-    used = sides * rest
-    far = jnp.concatenate(
-        [folded[:, :, :used], folded[:, :, half : half + used], last[:, :rest, :used]], axis=1
+    coarse, restricted = fused_kernel(
+        neighbours.T,
+        agg_map[None],
+        owners[None],
+        jnp.transpose(prolong, (1, 0, 2)),
+        jnp.transpose(jacobian, (1, 2, 0, 3)),
+        residual,
+        sizes,
     )
-    far = far.reshape(slots, width, sides, rest).transpose(0, 2, 1, 3)
-    heads = jnp.concatenate([head, below[:, :, :rest]], axis=2)
-    coarse = jnp.concatenate([heads, far], axis=3)
-    restricted = jnp.concatenate([below[:, 0, rest], last[:, rest, :rest]], axis=1)
-    return coarse, restricted
+    return jnp.transpose(coarse, (2, 0, 1, 3)), restricted
 
 
 def solution(mesh):

time: 71.3 us -> 52.3 us (0.73)
  other arithmetic: 10.6 us -> 0 us
  Pallas kernels: 52.1 us -> 47.3 us
  local copies, waits for them, and re-layouts: 7.24 us -> 4.04 us
    pallas_call x1, Pallas kernels: 52.1 us -> 47.3 us  [fused_kernel(): pl.pallas_call(kernel, in_specs=[pl.BlockSpec(memory_space=pltpu.VMEM)] *...]
    unnamed x3 -> x4, local copies, waits for them, and re-layouts: 0.03 us -> 4.04 us
    concatenate x4 -> x0, other arithmetic: 3.8 us -> none  [the longest x1 2.56 us: body(): coarse = jnp.concatenate([heads, far], axis=3)]
    slice x5 -> x0, local copies, waits for them, and re-layouts: 3.66 us -> none  [the longest x1 1.24 us: body(): head = rows[:, :tail].reshape(slots, sides, LANES, LANES)]
    reduce_sum x9 -> x0, other arithmetic: 3.19 us -> none  [the longest x1 1.01 us: tables(): position = jnp.sum(lower.astype(jnp.int32), axis=2)]
    transpose x1 -> x0, local copies, waits for them, and re-layouts: 1.82 us -> none  [body(): far = far.reshape(slots, width, sides, rest).transpose(0, 2, 1, 3)]
    reshape x2 -> x0, local copies, waits for them, and re-layouts: 1.54 us -> none  [the longest x1 0.82 us: body(): below = rows[:, tail:tail + sides * 8].reshape(slots, sides, 8, LANES)]
    add x4 -> x0, other arithmetic: 1.43 us -> none  [the longest x1 0.73 us: tables(): s_code = ids + elems * index]
where the time goes in v1:
time: 52.3 us; the launch traced here: 52 us
  Pallas kernels  47.3 us (90%)
  local copies, waits for them, and re-layouts  4.04 us (8%)
  between operations  0.65 us (1%)
    pallas_call x1, Pallas kernels, fused_kernel(): pl.pallas_call(kernel, in_specs=[pl.BlockSpec(memory_space=pltpu.VMEM)] *...  47.3 us
    unnamed x4, local copies, waits for them, and re-layouts  4.04 us

profile of v1, /device:TPU:0, one launch (start us, length us, event | category | flops | bytes accessed | tf_op | source)
XLA Modules:
  0.0 52.0 jit_solution(11573587444287284270)
XLA Ops:
  0.6 47.3 %shard_map.77 = (bf16[7,135,4,135]{3,2,1,0:T(4,128)(2,1)}, bf16[4,135]{1,0:T(4,128)(2,1)}) custom-call(s32[6,32]{1,0:T(8,128)} %bitcast.9, s32[1,32]{1,0:T(1,128)} %bitcast.10, s32[1,4]{1,0:T(1,128)} %bitcast.11, bf16[135,32,135]{2,1,0:T(8,128)(2,1)} %bitcast.7, bf16[7,135,32,135]{3,2,1,0:T(8,128)(2,1)} %bitcast.6, bf16[32,135]{1,0:T(8,128)(2,1)} %res_ref.1), custom_call_target="tpu_custom_call" | custom-call | tf_op jit(solution)/shard_map/pallas_call | solution.py:512
  47.9 0.0 copy-start
  47.9 3.5 %copy.10 = bf16[4,7,135,135]{3,0,2,1:T(4,128)(2,1)} copy(bf16[4,7,135,135]{3,0,2,1:T(4,128)(2,1)} %bitcast.8) | data formatting | bytes 2041200
  51.4 0.0 copy-done
  51.4 0.6 %copy.11 = bf16[4,135]{1,0:T(4,128)(2,1)} copy(bf16[4,135]{1,0:T(4,128)(2,1)S(1)} %copy-done) | data formatting | bytes 2160
Async XLA Ops:
  47.9 3.5 %copy-start = (bf16[4,135]{1,0:T(4,128)(2,1)S(1)}, bf16[4,135]{1,0:T(4,128)(2,1)}, u32[]{:S(2)}) copy-start(bf16[4,135]{1,0:T(4,128)(2,1)} %get-tuple-element.9) | copy-start | bytes 3244

commit v2 on v1

--- a/solution.py
+++ b/solution.py
@@ -119,6 +119,11 @@
                 expected = expected + exists.astype(jnp.int32)
 
         msg_far[...] = jnp.zeros_like(msg_far)
+        for sub in range(per_owner):
+            for piece, slot in ((5, sub), (6, out_slots - per_owner + sub)):
+                rows_ref[slot, piece * LANES : (piece + 1) * LANES, :] = jnp.zeros(
+                    (LANES, LANES), rows_ref.dtype
+                )
         pool[zero_block] = jnp.zeros(pool.shape[1:], pool.dtype)
 
         def spread(load, last):
@@ -312,11 +317,13 @@
             )
 
         def send_row(r, piece):
-            @pl.when(target_of(r) != me_z)
+            sent = present(piece, me_z)
+
+            @pl.when((target_of(r) != me_z) & sent)
             def _():
                 row_copy(r, piece).start()
 
-            @pl.when(target_of(r) == me_z)
+            @pl.when((target_of(r) == me_z) & sent)
             def _():
                 self_copy(r, piece).start()
 
@@ -324,7 +331,13 @@
             msg[r, s * LANES : (s + 1) * LANES, :] = value[:LANES, :LANES].astype(msg.dtype)
             msg_rem[r, s * 8 : (s + 1) * 8, :] = value[LANES:tall, :LANES]
             msg_far[r, :, s * rest : (s + 1) * rest] = value[:, LANES:width]
-            send_row(r, s)
+
+        def present(piece, z):
+            if piece == 5:
+                return z > 0
+            if piece == 6:
+                return z < size_z - 1
+            return True
 
         def side_sum(r, d):
             total = None
@@ -340,11 +353,11 @@
             acc[...] = jnp.zeros_like(acc)
             racc[...] = jnp.zeros_like(racc)
 
-            @pl.loop(0, members // 2)
+            @pl.loop(0, members // 4)
             def _(pair):
                 total = None
-                for u in range(2):
-                    code = table_ref[nch, r * members + pair * 2 + u]
+                for u in range(4):
+                    code = table_ref[nch, r * members + pair * 4 + u]
                     e, code = code % elems, code // elems
                     product = mul(jm[0, e], pool[e])
                     for axis in range(3):
@@ -360,15 +373,15 @@
             spare = lax.broadcasted_iota(jnp.int32, below.shape, 0) == width - LANES
             acc[LANES:tall, :] += jnp.where(spare, below, 0.0)
             emit(r, 0, acc[...])
-
-        def send_tail(r):
+            send_row(r, 0)
+
+        def pack_row_tail(r):
             msg_rem[r, sides * 8 : (sides + 1) * 8, :] = msg_far[r, LANES:tall, :]
             msg[r, tail : tail + half, :] = msg_rem[r].astype(msg.dtype)
             right = pltpu.roll(msg_far[r, half:LANES, :], half, 1)
             left = msg_far[r, :half, :]
             folded = jnp.where(lane_ids(left.shape) < half, left, right)
             msg[r, tail + half : msg_rows, :] = folded.astype(msg.dtype)
-            send_row(r, sides)
 
         @pl.loop(0, 2)
         def _(part):
@@ -383,10 +396,15 @@
 
                 @pl.loop(first, last)
                 def _(r, axis=axis):
-                    for d in (2 * axis, 2 * axis + 1):
-                        emit(r, 1 + d, side_sum(r, d))
+                    pair = (2 * axis, 2 * axis + 1)
+                    for d, total in [(d, side_sum(r, d)) for d in pair]:
+                        emit(r, 1 + d, total)
                     if axis == 2:
-                        send_tail(r)
+                        pack_row_tail(r)
+                    for d in pair:
+                        send_row(r, 1 + d)
+                    if axis == 2:
+                        send_row(r, sides)
 
         owner = me_z % stride_z == 0
 
@@ -403,6 +421,9 @@
 
         def arrive(piece):
             for slot in range(out_slots):
+                sent = present(piece, slot // per_owner)
+                if sent is False:
+                    continue
                 mine = slot // per_owner == me_z
 
                 @pl.when(mine)
@@ -442,11 +463,14 @@
                 at = sides * 8 + rest
                 mixed_rest[slot : slot + 1, LANES:] = below[at : at + 1, :rest]
             rest_ref[...] = mixed_rest[:out_slots].astype(rest_ref.dtype)
-            right = gathered(mixed, tall)
             for s in range(sides):
                 low = gathered(mixed_rem.at[s], 8)
                 out_ref[s, LANES:, :, :LANES] = low[:rest]
-                out_ref[s, :, :, LANES:] = right[:width, :, s * rest : (s + 1) * rest]
+                right = mixed[...]
+                if s > 0:
+                    right = pltpu.roll(right, LANES - s * rest, 1)
+                right = right.astype(jnp.bfloat16).reshape(tall, out_slots, LANES)
+                out_ref[s, :, :, LANES:] = right[:width, :, :rest]
 
         if stride_z == 1:
             unpack()
@@ -470,7 +494,10 @@
             @pl.when(target_of(r) != me_z)
             def _():
                 for piece in range(pieces):
-                    row_copy(r, piece).wait_send()
+
+                    @pl.when(present(piece, me_z))
+                    def _(piece=piece):
+                        row_copy(r, piece).wait_send()
 
     bf16, f32 = jnp.bfloat16, jnp.float32
     spread_rows = (width + 1) * pitch
@@ -516,14 +543,38 @@
         + [pl.BlockSpec(memory_space=pltpu.VMEM)],
         out_specs=[pl.BlockSpec(memory_space=pltpu.VMEM)] * 2,
         out_shape=[
-            jax.ShapeDtypeStruct((sides, width, out_slots, width), bf16),
-            jax.ShapeDtypeStruct((out_slots, width), bf16),
+            pltpu.VMEM((sides, width, out_slots, width), bf16),
+            pltpu.VMEM((out_slots, width), bf16),
         ],
         scratch_shapes=scratch,
         compiler_params=pltpu.CompilerParams(
-            collective_id=0, has_side_effects=True, vmem_limit_bytes=62 << 20
+            collective_id=0, has_side_effects=True, vmem_limit_bytes=54 << 20
         ),
     )(neighbours, agg_map, owners, prolong, jac, residual)
+
+
+def stored(coarse, restricted):
+    pieces = coarse.shape[0]
+
+    def kernel(coarse_ref, small_ref, out_hbm, small_hbm, sems):
+        copies = [
+            pltpu.make_async_copy(coarse_ref.at[k], out_hbm.at[k], sems.at[k])
+            for k in range(pieces)
+        ]
+        copies.append(pltpu.make_async_copy(small_ref, small_hbm, sems.at[pieces]))
+        for copy in copies:
+            copy.start()
+        for copy in copies:
+            copy.wait()
+
+    return pl.pallas_call(
+        kernel,
+        in_specs=[pl.BlockSpec(memory_space=pltpu.VMEM)] * 2,
+        out_specs=[pl.BlockSpec(memory_space=pl.ANY)] * 2,
+        out_shape=[jax.ShapeDtypeStruct(a.shape, a.dtype) for a in (coarse, restricted)],
+        scratch_shapes=[pltpu.SemaphoreType.DMA((pieces + 1,))],
+        compiler_params=pltpu.CompilerParams(vmem_limit_bytes=1 << 20),
+    )(coarse, restricted)
 
 
 def write_table(tab, nbr, agg, owners, base, mine, x, sizes):
@@ -632,6 +683,7 @@
         residual,
         sizes,
     )
+    coarse, restricted = stored(coarse, restricted)
     return jnp.transpose(coarse, (2, 0, 1, 3)), restricted
 
 

time: 52.3 us -> 46 us (0.88)
  local copies, waits for them, and re-layouts: 4.04 us -> 0 us
  Pallas kernels: 47.3 us -> 45.1 us
    unnamed x4 -> x0, local copies, waits for them, and re-layouts: 4.04 us -> none
    pallas_call x1, Pallas kernels: 47.3 us -> 43.8 us  [fused_kernel(): pl.pallas_call(kernel, in_specs=[pl.BlockSpec(memory_space=pltpu.VMEM)] *...]
    pallas_call x0 -> x1, Pallas kernels: none -> 1.33 us  [stored(): pl.pallas_call(kernel, in_specs=[pl.BlockSpec(memory_space=pltpu.VMEM)] *...]
where the time goes in v2:
time: 46 us; the launch traced here: 45.7 us
  Pallas kernels  45.1 us (98%)
  between operations  0.64 us (1%)
    pallas_call x1, Pallas kernels, fused_kernel(): pl.pallas_call(kernel, in_specs=[pl.BlockSpec(memory_space=pltpu.VMEM)] *...  43.8 us
    pallas_call x1, Pallas kernels, stored(): pl.pallas_call(kernel, in_specs=[pl.BlockSpec(memory_space=pltpu.VMEM)] *...  1.33 us

profile of v2, /device:TPU:0, one launch (start us, length us, event | category | flops | bytes accessed | tf_op | source)
XLA Modules:
  0.0 45.7 jit_solution(12133972878149631745)
XLA Ops:
  0.6 43.8 %shard_map.77 = (bf16[7,135,4,135]{3,2,1,0:T(4,128)(2,1)S(1)}, bf16[4,135]{1,0:T(4,128)(2,1)S(1)}) custom-call(s32[6,32]{1,0:T(8,128)} %bitcast.8, s32[1,32]{1,0:T(1,128)} %bitcast.9, s32[1,4]{1,0:T(1,128)} %bitcast.10, bf16[135,32,135]{2,1,0:T(8,128)(2,1)} %bitcast.7, bf16[7,135,32,135]{3,2,1,0:T(8,128)(2,1)} %bitcast.6, bf16[32,135]{1,0:T(8,128)(2,1)} %res_ref.1), custom_call_target="tpu_custom_call" | custom-call | tf_op jit(solution)/shard_map/pallas_call | solution.py:539
  44.4 1.3 %shard_map.78 = (bf16[7,135,4,135]{3,2,1,0:T(4,128)(2,1)}, bf16[4,135]{1,0:T(4,128)(2,1)}) custom-call(bf16[7,135,4,135]{3,2,1,0:T(4,128)(2,1)S(1)} %get-tuple-element.6.coarse_ref, bf16[4,135]{1,0:T(4,128)(2,1)S(1)} %get-tuple-element.7.small_ref), custom_call_target="tpu_custom_call" | custom-call | tf_op jit(solution)/shard_map/pallas_call | solution.py:570

commit v3 on v2

--- a/solution.py
+++ b/solution.py
@@ -47,8 +47,11 @@
 
 def partner_bits(me, r):
     high, low = me // 2, me % 2
-    high = high + (1 - r // 2) * (1 - 2 * high)
-    low = low + (1 - r % 2) * (1 - 2 * low)
+    inner = (high + low) % 2
+    cross = 1 - r // 2
+    turn = (1 + r + inner * cross) % 2
+    high = high + cross * (1 - 2 * high)
+    low = low + turn * (1 - 2 * low)
     return high * 2 + low
 
 
@@ -91,9 +94,14 @@
         p_copy = pltpu.make_async_copy(p_hbm, praw, p_sem)
         p_copy.start()
 
-        def j_copy(k):
-            slot = k % AHEAD
-            return pltpu.make_async_copy(j_hbm.at[k], jraw.at[slot], j_sem.at[slot])
+        def block_at(i):
+            return (i + 1) * (i < 2) + i * (i > 2)
+
+        def j_copy(i):
+            slot = i % AHEAD
+            return pltpu.make_async_copy(
+                j_hbm.at[block_at(i)], jraw.at[slot], j_sem.at[slot]
+            )
 
         barrier = pltpu.get_barrier_semaphore()
         for step in range(1, size_z):
@@ -269,18 +277,18 @@
                 e = group * 4 + u
                 pt[e] = block(e).T[:tall].astype(pt.dtype)
 
-        @pl.loop(0, sides)
-        def _(k):
-            j_copy(k).wait()
+        def lay_out(i):
+            k = block_at(i)
+            j_copy(i).wait()
             own = (k == 0).astype(jnp.float32)
             spread(
-                lambda c: jraw[k % AHEAD, pl.ds(c * step_rows, step_rows)],
+                lambda c: jraw[i % AHEAD, pl.ds(c * step_rows, step_rows)],
                 res_ref[...].astype(jnp.float32) * own,
             )
 
-            @pl.when(k + AHEAD < sides)
+            @pl.when(i + AHEAD < sides)
             def _():
-                j_copy(k + AHEAD).start()
+                j_copy(i + AHEAD).start()
 
             @pl.loop(0, elems // 4)
             def _(group):
@@ -383,28 +391,42 @@
             folded = jnp.where(lane_ids(left.shape) < half, left, right)
             msg[r, tail + half : msg_rows, :] = folded.astype(msg.dtype)
 
+        def side_slots(r, axis):
+            pair = (2 * axis, 2 * axis + 1)
+            for d, total in [(d, side_sum(r, d)) for d in pair]:
+                emit(r, 1 + d, total)
+            if axis == 2:
+                pack_row_tail(r)
+            for d in pair:
+                send_row(r, 1 + d)
+            if axis == 2:
+                send_row(r, sides)
+
+        axis_faces = [list(range(4, nch)), [2, 3], [0, 1]]
+
         @pl.loop(0, 2)
         def _(part):
             first, last = part * early, part * early + early
+
+            @pl.when(part == 0)
+            def _():
+                pl.loop(0, 2)(lay_out)
+                take_faces(axis_faces[0])
+
+            pl.loop(first, last)(lambda r: side_slots(r, 0))
+
+            @pl.when(part == 0)
+            def _():
+                pl.loop(2, sides)(lay_out)
+
             pl.loop(first, last)(own_slot)
-            axis_faces = [list(range(4, nch)), [2, 3], [0, 1]]
-            for axis in range(3):
+            for axis in (1, 2):
 
                 @pl.when(part == 0)
                 def _(axis=axis):
                     take_faces(axis_faces[axis])
 
-                @pl.loop(first, last)
-                def _(r, axis=axis):
-                    pair = (2 * axis, 2 * axis + 1)
-                    for d, total in [(d, side_sum(r, d)) for d in pair]:
-                        emit(r, 1 + d, total)
-                    if axis == 2:
-                        pack_row_tail(r)
-                    for d in pair:
-                        send_row(r, 1 + d)
-                    if axis == 2:
-                        send_row(r, sides)
+                pl.loop(first, last)(lambda r, axis=axis: side_slots(r, axis))
 
         owner = me_z % stride_z == 0
 
@@ -443,7 +465,7 @@
             return value.reshape(count, out_slots, LANES)
 
         def unpack():
-            for s in range(sides):
+            for s in [1, 2, 0, *range(3, sides)]:
                 arrive(s)
                 for slot in range(out_slots):
                     block_of = rows_ref[slot, s * LANES : (s + 1) * LANES, :]
@@ -619,7 +641,9 @@
     a_down = lax.broadcasted_iota(jnp.int32, (aggs_here, aggs_here), 0)
     a_along = lax.broadcasted_iota(jnp.int32, (aggs_here, aggs_here), 1)
     to = owners // stride_z
-    turn = 3 - (2 * jnp.abs(to // 2 - mine // 2) + jnp.abs(to % 2 - mine % 2))
+    crosses = jnp.abs(to // 2 - mine // 2)
+    flips = jnp.abs(to % 2 - mine % 2)
+    turn = 2 * (1 - crosses) + (1 + flips + crosses * ((mine // 2 + mine % 2) % 2)) % 2
     turn = jnp.broadcast_to(turn, a_down.shape)
     turn = by_row(jnp.where(a_down == a_along, turn, 0))
     if per_owner > 1:

time: 46 us -> 44.7 us (0.972)
  Pallas kernels: 45.1 us -> 43.8 us
    pallas_call x1, Pallas kernels: 43.8 us -> 42.5 us  [fused_kernel(): pl.pallas_call(kernel, in_specs=[pl.BlockSpec(memory_space=pltpu.VMEM)] *...]
where the time goes in v3:
time: 44.7 us; the launch traced here: 44.5 us
  Pallas kernels  43.8 us (98%)
  between operations  0.64 us (1%)
    pallas_call x1, Pallas kernels, fused_kernel(): pl.pallas_call(kernel, in_specs=[pl.BlockSpec(memory_space=pltpu.VMEM)] *...  42.5 us
    pallas_call x1, Pallas kernels, stored(): pl.pallas_call(kernel, in_specs=[pl.BlockSpec(memory_space=pltpu.VMEM)] *...  1.33 us

profile of v3, /device:TPU:0, one launch (start us, length us, event | category | flops | bytes accessed | tf_op | source)
XLA Modules:
  0.0 44.5 jit_solution(10556515708026613500)
XLA Ops:
  0.6 42.5 %shard_map.77 = (bf16[7,135,4,135]{3,2,1,0:T(4,128)(2,1)S(1)}, bf16[4,135]{1,0:T(4,128)(2,1)S(1)}) custom-call(s32[6,32]{1,0:T(8,128)} %bitcast.8, s32[1,32]{1,0:T(1,128)} %bitcast.9, s32[1,4]{1,0:T(1,128)} %bitcast.10, bf16[135,32,135]{2,1,0:T(8,128)(2,1)} %bitcast.7, bf16[7,135,32,135]{3,2,1,0:T(8,128)(2,1)} %bitcast.6, bf16[32,135]{1,0:T(8,128)(2,1)} %res_ref.1), custom_call_target="tpu_custom_call" | custom-call | tf_op jit(solution)/shard_map/pallas_call | solution.py:561
  43.1 1.3 %shard_map.78 = (bf16[7,135,4,135]{3,2,1,0:T(4,128)(2,1)}, bf16[4,135]{1,0:T(4,128)(2,1)}) custom-call(bf16[7,135,4,135]{3,2,1,0:T(4,128)(2,1)S(1)} %get-tuple-element.6.coarse_ref, bf16[4,135]{1,0:T(4,128)(2,1)S(1)} %get-tuple-element.7.small_ref), custom_call_target="tpu_custom_call" | custom-call | tf_op jit(solution)/shard_map/pallas_call | solution.py:592

commit v4 on v3

--- a/solution.py
+++ b/solution.py
@@ -86,7 +86,7 @@
         refs = refs[9 + 2 * nch :]
         remf, farf, msg, msg_rem, msg_far, racc, acc = refs[:7]
         rows_ref, mixed, mixed_rem, mixed_rest = refs[7:11]
-        t_sem, p_sem, j_sem, f_send, f_recv, r_send, r_recv, self_sem = refs[11:]
+        t_sem, p_sem, j_sem, f_send, f_recv, r_send, r_recv, self_sem, relay_sem = refs[11:]
         me = {"gx": lax.axis_index("gx"), "gy": lax.axis_index("gy"), "gz": lax.axis_index("gz")}
         size = {"gx": size_x, "gy": size_y, "gz": size_z}
         me_z = me["gz"]
@@ -104,16 +104,13 @@
             )
 
         barrier = pltpu.get_barrier_semaphore()
-        for step in range(1, size_z):
-            to = lax.rem(me_z + step, size_z)
-            pl.semaphore_signal(barrier, inc=1, device_id={"gz": to}, device_id_type=MESH)
-        expected = size_z - 1
+        expected = 0
         if size_x == 2:
             pl.semaphore_signal(
                 barrier, inc=1, device_id={"gx": 1 - me["gx"]}, device_id_type=MESH
             )
             expected = expected + 1
-        for axis in ["gy"] + (["gx"] if size_x > 2 else []):
+        for axis in ["gz", "gy"] + (["gx"] if size_x > 2 else []):
             for step in (1, -1):
                 there = me[axis] + step
                 exists = (there >= 0) & (there < size[axis])
@@ -182,7 +179,6 @@
                 pool[e] = block(e)[:, :width].astype(pool.dtype)
 
         t_copy.wait()
-        pl.semaphore_wait(barrier, expected)
 
         def face_target(c):
             axis, step, _, _ = channels[c]
@@ -230,16 +226,16 @@
             sends[c][at : at + count * 8, :] = remf[c, : count * 8, :].astype(jnp.bfloat16)
             sends[c][at + count * 8 : at + count * 8 + full, :] = farf[c].astype(jnp.bfloat16)
 
+        def pack_faces(group):
+            for c in group:
+                for n in range(channels[c][2]):
+                    pack(c, n)
+                pack_tail(c)
+
         def send_faces(group):
-            parts = max(len(face_parts(c)) for c in group)
-            for part in range(parts):
+            for part in range(max(len(face_parts(c)) for c in group)):
                 for c in group:
                     if part < len(face_parts(c)):
-                        if part < len(face_parts(c)) - 1:
-                            for n in range(part * CHUNK, (part + 1) * CHUNK):
-                                pack(c, n)
-                        else:
-                            pack_tail(c)
 
                         @when_sent(c)
                         def _(c=c, part=part):
@@ -268,6 +264,8 @@
                             c, :, n * rest : (n + 1) * rest
                         ].astype(pool.dtype)
 
+        pack_faces(list(range(nch)))
+        pl.semaphore_wait(barrier, expected)
         send_faces([0, 1])
         send_faces(list(range(2, nch)))
 
@@ -403,6 +401,24 @@
                 send_row(r, sides)
 
         axis_faces = [list(range(4, nch)), [2, 3], [0, 1]]
+
+        for step in range(size_z - 2):
+            for way, ahead in enumerate((1, -1)):
+                told = (me_z - ahead, me_z + ahead * (1 + step), me_z + ahead * (2 + step))
+                inside = [(z >= 0) & (z < size_z) for z in told]
+
+                @pl.when(inside[0] & inside[1])
+                def _(way=way, step=step, ahead=ahead):
+                    pl.semaphore_signal(
+                        relay_sem.at[way, step],
+                        inc=1,
+                        device_id={"gz": me_z - ahead},
+                        device_id_type=MESH,
+                    )
+
+                @pl.when(inside[2])
+                def _(way=way, step=step):
+                    pl.semaphore_wait(relay_sem.at[way, step], 1)
 
         @pl.loop(0, 2)
         def _(part):
@@ -557,6 +573,7 @@
         pltpu.SemaphoreType.DMA((aggs_here, pieces)),
         pltpu.SemaphoreType.DMA((out_slots, pieces)),
         pltpu.SemaphoreType.DMA((per_owner, pieces)),
+        pltpu.SemaphoreType.REGULAR((2, size_z - 2)),
     ]
     return pl.pallas_call(
         kernel,

time: 44.7 us -> 46 us (1.029)
  the two profiles are of different devices: /device:TPU:0 before, /device:TPU:30 now
where the time goes in v4:
time: 46 us; the launch traced here: 45.8 us
  Pallas kernels  45.1 us (98%)
  between operations  0.64 us (1%)
    pallas_call x1, Pallas kernels, fused_kernel(): pl.pallas_call(kernel, in_specs=[pl.BlockSpec(memory_space=pltpu.VMEM)] *...  43.8 us
    pallas_call x1, Pallas kernels, stored(): pl.pallas_call(kernel, in_specs=[pl.BlockSpec(memory_space=pltpu.VMEM)] *...  1.33 us

profile of v4, /device:TPU:30, one launch (start us, length us, event | category | flops | bytes accessed | tf_op | source)
XLA Modules:
  0.0 45.8 jit_solution(14432611114335369231)
XLA Ops:
  0.6 43.8 %shard_map.77 = (bf16[7,135,4,135]{3,2,1,0:T(4,128)(2,1)S(1)}, bf16[4,135]{1,0:T(4,128)(2,1)S(1)}) custom-call(s32[6,32]{1,0:T(8,128)} %bitcast.8, s32[1,32]{1,0:T(1,128)} %bitcast.9, s32[1,4]{1,0:T(1,128)} %bitcast.10, bf16[135,32,135]{2,1,0:T(8,128)(2,1)} %bitcast.7, bf16[7,135,32,135]{3,2,1,0:T(8,128)(2,1)} %bitcast.6, bf16[32,135]{1,0:T(8,128)(2,1)} %res_ref.1), custom_call_target="tpu_custom_call" | custom-call | tf_op jit(solution)/shard_map/pallas_call | solution.py:578
  44.4 1.3 %shard_map.78 = (bf16[7,135,4,135]{3,2,1,0:T(4,128)(2,1)}, bf16[4,135]{1,0:T(4,128)(2,1)}) custom-call(bf16[7,135,4,135]{3,2,1,0:T(4,128)(2,1)S(1)} %get-tuple-element.6.coarse_ref, bf16[4,135]{1,0:T(4,128)(2,1)S(1)} %get-tuple-element.7.small_ref), custom_call_target="tpu_custom_call" | custom-call | tf_op jit(solution)/shard_map/pallas_call | solution.py:609

commit v5 on v4

--- a/solution.py
+++ b/solution.py
@@ -226,15 +226,14 @@
             sends[c][at : at + count * 8, :] = remf[c, : count * 8, :].astype(jnp.bfloat16)
             sends[c][at + count * 8 : at + count * 8 + full, :] = farf[c].astype(jnp.bfloat16)
 
-        def pack_faces(group):
-            for c in group:
-                for n in range(channels[c][2]):
-                    pack(c, n)
-                pack_tail(c)
-
         def send_faces(group):
             for part in range(max(len(face_parts(c)) for c in group)):
                 for c in group:
+                    if part < len(face_parts(c)) - 1:
+                        for n in range(part * CHUNK, (part + 1) * CHUNK):
+                            pack(c, n)
+                    elif part < len(face_parts(c)):
+                        pack_tail(c)
                     if part < len(face_parts(c)):
 
                         @when_sent(c)
@@ -264,7 +263,6 @@
                             c, :, n * rest : (n + 1) * rest
                         ].astype(pool.dtype)
 
-        pack_faces(list(range(nch)))
         pl.semaphore_wait(barrier, expected)
         send_faces([0, 1])
         send_faces(list(range(2, nch)))

time: 46 us -> 45 us (0.978)
  the two profiles are of different devices: /device:TPU:30 before, /device:TPU:0 now
where the time goes in v5:
time: 45 us; the launch traced here: 44.7 us
  Pallas kernels  44.1 us (98%)
  between operations  0.64 us (1%)
    pallas_call x1, Pallas kernels, fused_kernel(): pl.pallas_call(kernel, in_specs=[pl.BlockSpec(memory_space=pltpu.VMEM)] *...  42.7 us
    pallas_call x1, Pallas kernels, stored(): pl.pallas_call(kernel, in_specs=[pl.BlockSpec(memory_space=pltpu.VMEM)] *...  1.33 us

profile of v5, /device:TPU:0, one launch (start us, length us, event | category | flops | bytes accessed | tf_op | source)
XLA Modules:
  0.0 44.7 jit_solution(6336272369871296573)
XLA Ops:
  0.6 42.7 %shard_map.77 = (bf16[7,135,4,135]{3,2,1,0:T(4,128)(2,1)S(1)}, bf16[4,135]{1,0:T(4,128)(2,1)S(1)}) custom-call(s32[6,32]{1,0:T(8,128)} %bitcast.8, s32[1,32]{1,0:T(1,128)} %bitcast.9, s32[1,4]{1,0:T(1,128)} %bitcast.10, bf16[135,32,135]{2,1,0:T(8,128)(2,1)} %bitcast.7, bf16[7,135,32,135]{3,2,1,0:T(8,128)(2,1)} %bitcast.6, bf16[32,135]{1,0:T(8,128)(2,1)} %res_ref.1), custom_call_target="tpu_custom_call" | custom-call | tf_op jit(solution)/shard_map/pallas_call | solution.py:576
  43.4 1.3 %shard_map.78 = (bf16[7,135,4,135]{3,2,1,0:T(4,128)(2,1)}, bf16[4,135]{1,0:T(4,128)(2,1)}) custom-call(bf16[7,135,4,135]{3,2,1,0:T(4,128)(2,1)S(1)} %get-tuple-element.6.coarse_ref, bf16[4,135]{1,0:T(4,128)(2,1)S(1)} %get-tuple-element.7.small_ref), custom_call_target="tpu_custom_call" | custom-call | tf_op jit(solution)/shard_map/pallas_call | solution.py:607

commit v6 on v5

--- a/solution.py
+++ b/solution.py
@@ -80,19 +80,29 @@
     early = aggs_here // 2
     step_rows = 5 if width % 5 == 0 else 1
 
-    def kernel(nbr_ref, agg_ref, own_ref, p_hbm, j_hbm, res_ref, out_ref, rest_ref, *refs):
+    def kernel(nbr_in, agg_in, own_in, p_hbm, j_hbm, res_in, out_ref, tail_ref, *refs):
+        nbr_ref, agg_ref, own_ref, res_ref, picks, picks_ref = refs[:6]
+        refs = refs[6:]
         tab, table_ref, praw, jraw, near, far, pool, pt, jm = refs[:9]
         sends, recvs = refs[9 : 9 + nch], refs[9 + nch : 9 + 2 * nch]
         refs = refs[9 + 2 * nch :]
         remf, farf, msg, msg_rem, msg_far, racc, acc = refs[:7]
-        rows_ref, mixed, mixed_rem, mixed_rest = refs[7:11]
-        t_sem, p_sem, j_sem, f_send, f_recv, r_send, r_recv, self_sem, relay_sem = refs[11:]
+        rows_ref, mixed = refs[7:9]
+        in_sem, k_sem, t_sem, p_sem, j_sem, f_send, f_recv, r_send, r_recv, self_sem, relay_sem = refs[9:]
         me = {"gx": lax.axis_index("gx"), "gy": lax.axis_index("gy"), "gz": lax.axis_index("gz")}
         size = {"gx": size_x, "gy": size_y, "gz": size_z}
         me_z = me["gz"]
 
         p_copy = pltpu.make_async_copy(p_hbm, praw, p_sem)
         p_copy.start()
+        small = [
+            pltpu.make_async_copy(source, ref, in_sem.at[i])
+            for i, (source, ref) in enumerate(
+                zip((nbr_in, agg_in, own_in, res_in), (nbr_ref, agg_ref, own_ref, res_ref))
+            )
+        ]
+        for copy in small:
+            copy.start()
 
         def block_at(i):
             return (i + 1) * (i < 2) + i * (i > 2)
@@ -123,14 +133,6 @@
 
                 expected = expected + exists.astype(jnp.int32)
 
-        msg_far[...] = jnp.zeros_like(msg_far)
-        for sub in range(per_owner):
-            for piece, slot in ((5, sub), (6, out_slots - per_owner + sub)):
-                rows_ref[slot, piece * LANES : (piece + 1) * LANES, :] = jnp.zeros(
-                    (LANES, LANES), rows_ref.dtype
-                )
-        pool[zero_block] = jnp.zeros(pool.shape[1:], pool.dtype)
-
         def spread(load, last):
             @pl.loop(0, width // step_rows)
             def _(c):
@@ -152,18 +154,15 @@
             return jnp.concatenate([both, below], axis=0)
 
         device = (me["gx"] * size_y + me["gy"]) * size_z + me_z
-        write_table(
-            tab,
-            nbr_ref[...],
-            agg_ref[...] - device * aggs_here,
-            own_ref[...],
-            device * elems,
-            me_z // stride_z,
-            me["gx"],
-            sizes,
-        )
-        t_copy = pltpu.make_async_copy(tab, table_ref, t_sem)
-        t_copy.start()
+        for copy in small:
+            copy.wait()
+        lists = Lists(nbr_ref[...], device * elems)
+        for c in range(2):
+            picks[c : c + 1, :elems] = lists.side(channels[c][3])
+        k_copy = pltpu.make_async_copy(picks, picks_ref, k_sem)
+        k_copy.start()
+        for c in range(2):
+            farf[c, tall:, :] = jnp.zeros((full - tall, LANES), jnp.float32)
         p_copy.wait()
         for k in range(AHEAD):
             j_copy(k).start()
@@ -172,14 +171,6 @@
             jnp.zeros((elems, width), jnp.float32),
         )
 
-        @pl.loop(0, elems // 4)
-        def _(group):
-            for u in range(4):
-                e = group * 4 + u
-                pool[e] = block(e)[:, :width].astype(pool.dtype)
-
-        t_copy.wait()
-
         def face_target(c):
             axis, step, _, _ = channels[c]
             return {axis: 1 - me[axis] if step == 0 else me[axis] + step}
@@ -208,13 +199,30 @@
             return pltpu.make_async_remote_copy(
                 src_ref=sends[c].at[pl.ds(start, rows)],
                 dst_ref=recvs[c].at[pl.ds(start, rows)],
-                send_sem=f_send.at[c, part],
-                recv_sem=f_recv.at[c, part],
+                send_sem=f_send.at[c],
+                recv_sem=f_recv.at[c],
                 device_id=face_target(c),
                 device_id_type=MESH,
             )
 
+        def whole_face(c):
+            return pltpu.make_async_remote_copy(
+                src_ref=sends[c],
+                dst_ref=recvs[c],
+                send_sem=f_send.at[c],
+                recv_sem=f_recv.at[c],
+                device_id=face_target(c),
+                device_id_type=MESH,
+            )
+
         def pack(c, n):
+            if c < 2:
+                rows = pl.ds(picks_ref[c, n] % elems, width + 1, stride=pitch)
+                left, right = near[rows, :], far[rows, :]
+                sends[c][n * LANES : (n + 1) * LANES, :] = left[:LANES].astype(jnp.bfloat16)
+                remf[c, n * 8 : (n + 1) * 8, :] = left[LANES:tall]
+                farf[c, :tall, n * rest : (n + 1) * rest] = right[:, :rest]
+                return
             whole = pool[table_ref[c, n] % elems]
             sends[c][n * LANES : (n + 1) * LANES, :] = whole[:LANES, :LANES]
             remf[c, n * 8 : (n + 1) * 8, :] = whole[LANES:tall, :LANES].astype(jnp.float32)
@@ -245,8 +253,7 @@
 
                 @when_received(c)
                 def _(c=c):
-                    for part in range(len(face_parts(c))):
-                        face_copy(c, part).wait_recv()
+                    whole_face(c).wait_recv()
                     count = channels[c][2]
                     at = count * LANES
                     remf[c, : count * 8, :] = recvs[c][at : at + count * 8, :].astype(jnp.float32)
@@ -264,8 +271,30 @@
                         ].astype(pool.dtype)
 
         pl.semaphore_wait(barrier, expected)
+        k_copy.wait()
         send_faces([0, 1])
-        send_faces(list(range(2, nch)))
+
+        lists.table(
+            tab, agg_ref[...] - device * aggs_here, own_ref[...], me_z // stride_z, me["gx"], sizes
+        )
+        t_copy = pltpu.make_async_copy(tab, table_ref, t_sem)
+        t_copy.start()
+        msg_far[...] = jnp.zeros_like(msg_far)
+        for sub in range(per_owner):
+            for piece, slot in ((5, sub), (6, out_slots - per_owner + sub)):
+                rows_ref[slot, piece * LANES : (piece + 1) * LANES, :] = jnp.zeros(
+                    (LANES, LANES), rows_ref.dtype
+                )
+        pool[zero_block] = jnp.zeros(pool.shape[1:], pool.dtype)
+
+        @pl.loop(0, elems // 4)
+        def _(group):
+            for u in range(4):
+                e = group * 4 + u
+                pool[e] = block(e)[:, :width].astype(pool.dtype)
+
+        t_copy.wait()
+        send_faces([*range(4, nch), 2, 3])
 
         @pl.loop(0, elems // 4)
         def _(group):
@@ -300,24 +329,29 @@
         def slot_of(z, r):
             return z * per_owner + r % per_owner
 
+        def late(piece):
+            return int(piece > 4)
+
         def row_copy(r, piece):
             at = pl.ds(pl.multiple_of(piece * LANES, LANES), LANES)
             slot = slot_of(me_z, r)
+            last = piece == sides
             return pltpu.make_async_remote_copy(
                 src_ref=msg.at[r, at],
-                dst_ref=rows_ref.at[slot, at],
-                send_sem=r_send.at[r, piece],
-                recv_sem=r_recv.at[slot, piece],
+                dst_ref=tail_ref.at[slot] if last else rows_ref.at[slot, at],
+                send_sem=r_send.at[r],
+                recv_sem=r_recv.at[slot, late(piece)],
                 device_id={"gz": target_of(r)},
                 device_id_type=MESH,
             )
 
         def self_copy(r, piece):
             at = pl.ds(pl.multiple_of(piece * LANES, LANES), LANES)
+            slot = slot_of(me_z, r)
             return pltpu.make_async_copy(
                 msg.at[r, at],
-                rows_ref.at[slot_of(me_z, r), at],
-                self_sem.at[r % per_owner, piece],
+                tail_ref.at[slot] if piece == sides else rows_ref.at[slot, at],
+                self_sem.at[r % per_owner, late(piece)],
             )
 
         def send_row(r, piece):
@@ -444,69 +478,42 @@
 
         owner = me_z % stride_z == 0
 
-        def row_arrival(slot, piece):
-            at = pl.ds(piece * LANES, LANES)
-            return pltpu.make_async_remote_copy(
-                src_ref=msg.at[0, at],
-                dst_ref=rows_ref.at[slot, at],
-                send_sem=r_send.at[0, piece],
-                recv_sem=r_recv.at[slot, piece],
-                device_id={"gz": me_z},
-                device_id_type=MESH,
-            )
-
-        def arrive(piece):
+        def span(group, z):
+            start, count = (0, 5) if group == 0 else (5, pieces - 5)
+            if group == 1 and z in (0, size_z - 1):
+                count -= 1
+            return pl.ds(start * LANES, count * LANES)
+
+        def arrive(group):
             for slot in range(out_slots):
-                sent = present(piece, slot // per_owner)
-                if sent is False:
-                    continue
+                at = span(group, slot // per_owner)
                 mine = slot // per_owner == me_z
 
                 @pl.when(mine)
-                def _(slot=slot):
-                    self_copy(aggs_here - per_owner + slot % per_owner, piece).wait()
+                def _(slot=slot, at=at):
+                    pltpu.make_async_copy(
+                        msg.at[0, at], msg.at[1, at], self_sem.at[slot % per_owner, group]
+                    ).wait()
 
                 @pl.when(jnp.logical_not(mine))
-                def _(slot=slot):
-                    row_arrival(slot, piece).wait_recv()
-
-        def scatter(ref, slot, start, value):
-            count = value.shape[0]
-            ref[pl.ds(start * out_slots + slot, count, stride=out_slots), :] = value
-
-        def gathered(ref, count):
-            value = ref[: count * out_slots, :].astype(jnp.bfloat16)
-            return value.reshape(count, out_slots, LANES)
+                def _(slot=slot, at=at):
+                    pltpu.make_async_remote_copy(
+                        src_ref=msg.at[0, at],
+                        dst_ref=msg.at[0, at],
+                        send_sem=r_send.at[0],
+                        recv_sem=r_recv.at[slot, group],
+                        device_id={"gz": me_z},
+                        device_id_type=MESH,
+                    ).wait_recv()
 
         def unpack():
-            for s in [1, 2, 0, *range(3, sides)]:
-                arrive(s)
+            for s in range(sides):
+                if s in (0, 5):
+                    arrive(late(s))
                 for slot in range(out_slots):
                     block_of = rows_ref[slot, s * LANES : (s + 1) * LANES, :]
-                    scatter(mixed, slot, 0, block_of.astype(jnp.float32))
-                out_ref[s, :LANES, :, :LANES] = gathered(mixed, LANES)
-
-            arrive(sides)
-            for slot in range(out_slots):
-                below = rows_ref[slot, tail : tail + half, :].astype(jnp.float32)
-                folded = rows_ref[slot, tail + half : msg_rows, :].astype(jnp.float32)
-                scatter(mixed, slot, 0, folded)
-                scatter(mixed, slot, half, pltpu.roll(folded, half, 1))
-                scatter(mixed, slot, LANES, below[sides * 8 :])
-                for s in range(sides):
-                    scatter(mixed_rem.at[s], slot, 0, below[s * 8 : (s + 1) * 8])
-                mixed_rest[slot : slot + 1, :LANES] = below[rest : rest + 1]
-                at = sides * 8 + rest
-                mixed_rest[slot : slot + 1, LANES:] = below[at : at + 1, :rest]
-            rest_ref[...] = mixed_rest[:out_slots].astype(rest_ref.dtype)
-            for s in range(sides):
-                low = gathered(mixed_rem.at[s], 8)
-                out_ref[s, LANES:, :, :LANES] = low[:rest]
-                right = mixed[...]
-                if s > 0:
-                    right = pltpu.roll(right, LANES - s * rest, 1)
-                right = right.astype(jnp.bfloat16).reshape(tall, out_slots, LANES)
-                out_ref[s, :, :, LANES:] = right[:width, :, :rest]
+                    scatter(mixed, out_slots, slot, 0, block_of.astype(jnp.float32))
+                out_ref[s, :LANES, :, :LANES] = gathered(mixed[...], LANES, out_slots)
 
         if stride_z == 1:
             unpack()
@@ -516,31 +523,41 @@
             @pl.when(jnp.logical_not(owner))
             def _():
                 out_ref[...] = jnp.zeros_like(out_ref)
-                rest_ref[...] = jnp.zeros_like(rest_ref)
+                tail_ref[...] = jnp.zeros_like(tail_ref)
 
         for c in range(nch):
 
             @when_sent(c)
             def _(c=c):
-                for part in range(len(face_parts(c))):
-                    face_copy(c, part).wait_send()
+                whole_face(c).wait_send()
 
         @pl.loop(0, aggs_here)
         def _(r):
             @pl.when(target_of(r) != me_z)
             def _():
-                for piece in range(pieces):
-
-                    @pl.when(present(piece, me_z))
-                    def _(piece=piece):
-                        row_copy(r, piece).wait_send()
+                inside = (me_z > 0) & (me_z < size_z - 1)
+                for count, at_end in ((pieces, False), (pieces - 1, True)):
+
+                    @pl.when(inside != at_end)
+                    def _(count=count):
+                        at = pl.ds(0, count * LANES)
+                        pltpu.make_async_remote_copy(
+                            src_ref=msg.at[r, at],
+                            dst_ref=msg.at[r, at],
+                            send_sem=r_send.at[r],
+                            recv_sem=r_recv.at[0, 0],
+                            device_id={"gz": target_of(r)},
+                            device_id_type=MESH,
+                        ).wait_send()
 
     bf16, f32 = jnp.bfloat16, jnp.float32
     spread_rows = (width + 1) * pitch
     faces = [pltpu.VMEM((face_rows(count, full), LANES), bf16) for _, _, count, _ in channels]
-    parts = most // CHUNK + 1
     table_rows = pl.cdiv(nch + sides, 8) * 8
     scratch = [
+        *[pltpu.VMEM(a.shape, a.dtype) for a in (neighbours, agg_map, owners, residual)],
+        pltpu.VMEM((8, LANES), jnp.int32),
+        pltpu.SMEM((8, LANES), jnp.int32),
         pltpu.VMEM((table_rows, LANES), jnp.int32),
         pltpu.SMEM((table_rows, LANES), jnp.int32),
         pltpu.VMEM((width, elems, width), bf16),
@@ -559,29 +576,27 @@
         pltpu.VMEM((aggs_here, tall, LANES), f32),
         pltpu.VMEM((8, width), f32),
         pltpu.VMEM((tall, width), f32),
-        pltpu.VMEM((out_slots, msg_rows, LANES), bf16),
-        pltpu.VMEM((tall * out_slots, LANES), f32),
-        pltpu.VMEM((sides, 8 * out_slots, LANES), f32),
-        pltpu.VMEM((pl.cdiv(out_slots, 8) * 8, width), f32),
+        pltpu.VMEM((out_slots, tail, LANES), bf16),
+        pltpu.VMEM((LANES * out_slots, LANES), f32),
+        pltpu.SemaphoreType.DMA((4,)),
+        pltpu.SemaphoreType.DMA,
         pltpu.SemaphoreType.DMA,
         pltpu.SemaphoreType.DMA,
         pltpu.SemaphoreType.DMA((AHEAD,)),
-        pltpu.SemaphoreType.DMA((nch, parts)),
-        pltpu.SemaphoreType.DMA((nch, parts)),
-        pltpu.SemaphoreType.DMA((aggs_here, pieces)),
-        pltpu.SemaphoreType.DMA((out_slots, pieces)),
-        pltpu.SemaphoreType.DMA((per_owner, pieces)),
+        pltpu.SemaphoreType.DMA((nch,)),
+        pltpu.SemaphoreType.DMA((nch,)),
+        pltpu.SemaphoreType.DMA((aggs_here,)),
+        pltpu.SemaphoreType.DMA((out_slots, 2)),
+        pltpu.SemaphoreType.DMA((per_owner, 2)),
         pltpu.SemaphoreType.REGULAR((2, size_z - 2)),
     ]
     return pl.pallas_call(
         kernel,
-        in_specs=[pl.BlockSpec(memory_space=pltpu.VMEM)] * 3
-        + [pl.BlockSpec(memory_space=pl.ANY)] * 2
-        + [pl.BlockSpec(memory_space=pltpu.VMEM)],
+        in_specs=[pl.BlockSpec(memory_space=pl.ANY)] * 6,
         out_specs=[pl.BlockSpec(memory_space=pltpu.VMEM)] * 2,
         out_shape=[
             pltpu.VMEM((sides, width, out_slots, width), bf16),
-            pltpu.VMEM((out_slots, width), bf16),
+            pltpu.VMEM((out_slots, LANES, LANES), bf16),
         ],
         scratch_shapes=scratch,
         compiler_params=pltpu.CompilerParams(
@@ -590,31 +605,117 @@
     )(neighbours, agg_map, owners, prolong, jac, residual)
 
 
-def stored(coarse, restricted):
-    pieces = coarse.shape[0]
-
-    def kernel(coarse_ref, small_ref, out_hbm, small_hbm, sems):
-        copies = [
-            pltpu.make_async_copy(coarse_ref.at[k], out_hbm.at[k], sems.at[k])
-            for k in range(pieces)
-        ]
-        copies.append(pltpu.make_async_copy(small_ref, small_hbm, sems.at[pieces]))
-        for copy in copies:
-            copy.start()
+def scatter(ref, out_slots, slot, start, value):
+    count = value.shape[0]
+    ref[pl.ds(start * out_slots + slot, count, stride=out_slots), :] = value
+
+
+def gathered(value, count, out_slots):
+    return value.astype(jnp.bfloat16).reshape(count, out_slots, LANES)
+
+
+def stored(coarse, tails):
+    sides, width, out_slots, _ = coarse.shape
+    rest = width - LANES
+    half = LANES // 2
+    tall = pl.cdiv(width + 1, 8) * 8
+
+    def kernel(_, tail_ref, kept, out_hbm, small_hbm, mixed, mixed_rem, restr, small, sems):
+        for slot in range(out_slots):
+            below = tail_ref[slot, :half].astype(jnp.float32)
+            folded = tail_ref[slot, half:].astype(jnp.float32)
+            scatter(mixed, out_slots, slot, 0, folded)
+            scatter(mixed, out_slots, slot, half, pltpu.roll(folded, half, 1))
+            scatter(mixed, out_slots, slot, LANES, below[sides * 8 :])
+            for s in range(sides):
+                scatter(mixed_rem.at[s], out_slots, slot, 0, below[s * 8 : (s + 1) * 8])
+            restr[slot : slot + 1, :LANES] = below[rest : rest + 1]
+            at = sides * 8 + rest
+            restr[slot : slot + 1, LANES:] = below[at : at + 1, :rest]
+        small[...] = restr[:out_slots].astype(small.dtype)
+        copies = [pltpu.make_async_copy(small, small_hbm, sems.at[sides])]
+        copies[0].start()
+        for s in range(sides):
+            low = gathered(mixed_rem[s], 8, out_slots)
+            kept[s, LANES:, :, :LANES] = low[:rest]
+            right = mixed[...]
+            if s > 0:
+                right = pltpu.roll(right, LANES - s * rest, 1)
+            kept[s, :, :, LANES:] = gathered(right, tall, out_slots)[:width, :, :rest]
+            copies.append(pltpu.make_async_copy(kept.at[s], out_hbm.at[s], sems.at[s]))
+            copies[-1].start()
         for copy in copies:
             copy.wait()
 
-    return pl.pallas_call(
+    f32 = jnp.float32
+    _, out, small = pl.pallas_call(
         kernel,
         in_specs=[pl.BlockSpec(memory_space=pltpu.VMEM)] * 2,
-        out_specs=[pl.BlockSpec(memory_space=pl.ANY)] * 2,
-        out_shape=[jax.ShapeDtypeStruct(a.shape, a.dtype) for a in (coarse, restricted)],
-        scratch_shapes=[pltpu.SemaphoreType.DMA((pieces + 1,))],
-        compiler_params=pltpu.CompilerParams(vmem_limit_bytes=1 << 20),
-    )(coarse, restricted)
-
-
-def write_table(tab, nbr, agg, owners, base, mine, x, sizes):
+        out_specs=[pl.BlockSpec(memory_space=pltpu.VMEM)]
+        + [pl.BlockSpec(memory_space=pl.ANY)] * 2,
+        out_shape=[
+            pltpu.VMEM(coarse.shape, coarse.dtype),
+            jax.ShapeDtypeStruct(coarse.shape, coarse.dtype),
+            jax.ShapeDtypeStruct((out_slots, width), coarse.dtype),
+        ],
+        input_output_aliases={0: 0},
+        scratch_shapes=[
+            pltpu.VMEM((tall * out_slots, LANES), f32),
+            pltpu.VMEM((sides, 8 * out_slots, LANES), f32),
+            pltpu.VMEM((pl.cdiv(out_slots, 8) * 8, width), f32),
+            pltpu.VMEM((out_slots, width), coarse.dtype),
+            pltpu.SemaphoreType.DMA((sides + 1,)),
+        ],
+        compiler_params=pltpu.CompilerParams(vmem_limit_bytes=4 << 20),
+    )(coarse, tails)
+    return out, small
+
+
+class Lists:
+    def __init__(self, nbr, base):
+        self.nbr, self.base = nbr, base
+        square = (nbr.shape[1],) * 2
+        self.down = lax.broadcasted_iota(jnp.int32, square, 0)
+        self.along = lax.broadcasted_iota(jnp.int32, square, 1)
+        self.eye = flag(self.down == self.along)
+        self.before = flag(self.along < self.down)
+
+    def column(self, row):
+        return by_row(self.eye * row)
+
+    def row(self, col):
+        return by_column(self.eye * col)
+
+    def listed(self, place, value):
+        return by_column(flag(place == self.along) * value)
+
+    def side(self, d):
+        elems = self.nbr.shape[1]
+        local = self.nbr[d : d + 1] - self.base
+        away_row = 1 - flag(local >= 0) * flag(local < elems)
+        rank = by_row(self.before * away_row)
+        place = jnp.where(self.column(away_row) > 0, rank, -1)
+        return self.listed(place, self.down[:, :1])
+
+    def table(self, tab, agg, owners, mine, x, sizes):
+        write_table(self, tab, agg, owners, mine, x, sizes)
+
+
+def flag(mask):
+    return jnp.where(mask, 1, 0)
+
+
+def by_row(value):
+    return jnp.sum(value, axis=1, keepdims=True)
+
+
+def by_column(value):
+    return jnp.sum(value, axis=0, keepdims=True)
+
+
+def write_table(lists, tab, agg, owners, mine, x, sizes):
+    nbr, base = lists.nbr, lists.base
+    column, row, listed = lists.column, lists.row, lists.listed
     size_x, _, size_z = sizes
     elems, aggs_here = nbr.shape[1], owners.shape[1]
     per_owner = aggs_here // GROUPS
@@ -624,31 +725,8 @@
     channels = channels_of(size_x)
     offsets, zero_block = channel_offsets(channels, elems)
     nch = len(channels)
-    square = (elems, elems)
-    down = lax.broadcasted_iota(jnp.int32, square, 0)
-    along = lax.broadcasted_iota(jnp.int32, square, 1)
-    ids = down[:, :1]
-
-    def flag(mask):
-        return jnp.where(mask, 1, 0)
-
-    eye = flag(down == along)
-    before = flag(along < down)
-
-    def by_row(value):
-        return jnp.sum(value, axis=1, keepdims=True)
-
-    def by_column(value):
-        return jnp.sum(value, axis=0, keepdims=True)
-
-    def column(row):
-        return by_row(eye * row)
-
-    def row(col):
-        return by_column(eye * col)
-
-    def listed(place, value):
-        return by_column(flag(place == along) * value)
+    along, before = lists.along, lists.before
+    ids = lists.down[:, :1]
 
     def put(at, value):
         tab[at : at + 1, :elems] = value
@@ -673,21 +751,18 @@
     m_place = order * members + by_row(together)
 
     if size_x == 2:
-        listing = [(5, 0), (4, 1), (3, 2), (2, 3)]
+        listing = [(3, 2), (2, 3)]
         sources = [4, 4, 2, 3, 0, 1]
     else:
-        listing = [(5, 0), (4, 1), (3, 2), (2, 3), (1, 4), (0, 5)]
+        listing = [(3, 2), (2, 3), (1, 4), (0, 5)]
         sources = [4, 5, 2, 3, 0, 1]
-    sides_of, local_of, same_of = [], [], []
+    local_of, same_of = [], []
     for d in range(6):
         nbr_row = nbr[d : d + 1]
         nbr_col = column(nbr_row)
         local_row, local = nbr_row - base, nbr_col - base
         away_row = 1 - flag(local_row >= 0) * flag(local_row < elems)
         here = flag(local >= 0) * flag(local < elems)
-        rank = by_row(before * away_row)
-        place = jnp.where(here > 0, -1, rank)
-        sides_of.append(listed(place, ids))
         crossing = away_row * flag(nbr_row >= 0)
         position = by_row(crossing * flag(nbr_row < nbr_col))
         index = jnp.where(here > 0, local, position + offsets[sources[d]])
@@ -700,9 +775,9 @@
         s_place = jnp.where(same > 0, -1, order * on_face + s_rank)
         put(nch + 1 + d, listed(s_place, ids + elems * index))
     for d, c in listing:
-        put(c, sides_of[d])
+        put(c, lists.side(d))
     if size_x == 2:
-        put(4, jnp.where(x == 0, sides_of[1], sides_of[0]))
+        put(4, jnp.where(x == 0, lists.side(1), lists.side(0)))
     code = jnp.zeros_like(ids)
     for axis in (2, 1, 0):
         after = same_of[2 * axis + 1] > 0
@@ -713,7 +788,7 @@
 
 def body(jacobian, prolong, residual, neighbours, agg_map, owners):
     sizes = tuple(lax.axis_size(a) for a in ("gx", "gy", "gz"))
-    coarse, restricted = fused_kernel(
+    coarse, tails = fused_kernel(
         neighbours.T,
         agg_map[None],
         owners[None],
@@ -722,7 +797,7 @@
         residual,
         sizes,
     )
-    coarse, restricted = stored(coarse, restricted)
+    coarse, restricted = stored(coarse, tails)
     return jnp.transpose(coarse, (2, 0, 1, 3)), restricted
 
 

time: 45 us -> 43.8 us (0.973)
  Pallas kernels: 44.1 us -> 42.9 us
    pallas_call x1, Pallas kernels: 42.7 us -> 41.5 us  [fused_kernel(): pl.pallas_call(kernel, in_specs=[pl.BlockSpec(memory_space=pl.ANY)] * 6,...]
where the time goes in v6:
time: 43.8 us; the launch traced here: 43.5 us
  Pallas kernels  42.9 us (98%)
  between operations  0.64 us (1%)
    pallas_call x1, Pallas kernels, fused_kernel(): pl.pallas_call(kernel, in_specs=[pl.BlockSpec(memory_space=pl.ANY)] * 6,...  41.5 us
    pallas_call x1, Pallas kernels, stored(): pl.pallas_call(kernel, in_specs=[pl.BlockSpec(memory_space=pltpu.VMEM)] *...  1.44 us

profile of v6, /device:TPU:0, one launch (start us, length us, event | category | flops | bytes accessed | tf_op | source)
XLA Modules:
  0.0 43.5 jit_solution(2130374812898700669)
XLA Ops:
  0.6 41.5 %shard_map.77 = (bf16[7,135,4,135]{3,2,1,0:T(4,128)(2,1)S(1)}, bf16[4,128,128]{2,1,0:T(8,128)(2,1)S(1)}) custom-call(s32[6,32]{1,0:T(8,128)} %bitcast.8, s32[1,32]{1,0:T(1,128)} %bitcast.9, s32[1,4]{1,0:T(1,128)} %bitcast.10, bf16[135,32,135]{2,1,0:T(8,128)(2,1)} %bitcast.7, bf16[7,135,32,135]{3,2,1,0:T(8,128)(2,1)} %bitcast.6, bf16[32,135]{1,0:T(8,128)(2,1)} %res_in.1), custom_call_target="tpu_custom_call" | custom-call | tf_op jit(solution)/shard_map/pallas_call | solution.py:593
  42.1 1.4 %shard_map.78 = (bf16[7,135,4,135]{3,2,1,0:T(4,128)(2,1)S(1)}, bf16[7,135,4,135]{3,2,1,0:T(4,128)(2,1)}, bf16[4,135]{1,0:T(4,128)(2,1)}) custom-call(bf16[7,135,4,135]{3,2,1,0:T(4,128)(2,1)S(1)} %get-tuple-element.6._, bf16[4,128,128]{2,1,0:T(8,128)(2,1)S(1)} %get-tuple-element.7.tail_ref), custom_call_target="tpu_custom_call", output_to_operand_aliasing={{0}: (0, {})} | custom-call | tf_op jit(solution)/shard_map/pallas_call | solution.py:651

commit v7 on v6

--- a/solution.py
+++ b/solution.py
@@ -86,9 +86,9 @@
         tab, table_ref, praw, jraw, near, far, pool, pt, jm = refs[:9]
         sends, recvs = refs[9 : 9 + nch], refs[9 + nch : 9 + 2 * nch]
         refs = refs[9 + 2 * nch :]
-        remf, farf, msg, msg_rem, msg_far, racc, acc = refs[:7]
-        rows_ref, mixed = refs[7:9]
-        in_sem, k_sem, t_sem, p_sem, j_sem, f_send, f_recv, r_send, r_recv, self_sem, relay_sem = refs[9:]
+        remf, farf, msg, msg_rem, msg_far = refs[:5]
+        rows_ref, mixed = refs[5:7]
+        in_sem, k_sem, t_sem, p_sem, j_sem, f_send, f_recv, r_send, r_recv, self_sem, relay_sem = refs[7:]
         me = {"gx": lax.axis_index("gx"), "gy": lax.axis_index("gy"), "gz": lax.axis_index("gz")}
         size = {"gx": size_x, "gy": size_y, "gz": size_z}
         me_z = me["gz"]
@@ -296,10 +296,10 @@
         t_copy.wait()
         send_faces([*range(4, nch), 2, 3])
 
-        @pl.loop(0, elems // 4)
+        @pl.loop(0, elems // 8)
         def _(group):
-            for u in range(4):
-                e = group * 4 + u
+            for u in range(8):
+                e = group * 8 + u
                 pt[e] = block(e).T[:tall].astype(pt.dtype)
 
         def lay_out(i):
@@ -365,10 +365,13 @@
             def _():
                 self_copy(r, piece).start()
 
-        def emit(r, s, value):
+        def emit(r, s, value, more=0.0):
             msg[r, s * LANES : (s + 1) * LANES, :] = value[:LANES, :LANES].astype(msg.dtype)
-            msg_rem[r, s * 8 : (s + 1) * 8, :] = value[LANES:tall, :LANES]
-            msg_far[r, :, s * rest : (s + 1) * rest] = value[:, LANES:width]
+            last = value[LANES:tall] + more
+            msg_rem[r, s * 8 : (s + 1) * 8, :] = last[:, :LANES]
+            lanes = slice(s * rest, (s + 1) * rest)
+            msg_far[r, :LANES, lanes] = value[:LANES, LANES:width]
+            msg_far[r, LANES:, lanes] = last[:, LANES:width]
 
         def present(piece, z):
             if piece == 5:
@@ -388,29 +391,21 @@
             return total
 
         def own_slot(r):
-            acc[...] = jnp.zeros_like(acc)
-            racc[...] = jnp.zeros_like(racc)
-
-            @pl.loop(0, members // 4)
-            def _(pair):
-                total = None
-                for u in range(4):
-                    code = table_ref[nch, r * members + pair * 4 + u]
-                    e, code = code % elems, code // elems
-                    product = mul(jm[0, e], pool[e])
-                    for axis in range(3):
-                        x, code = code % (2 * elems), code // (2 * elems)
-                        k = 1 + 2 * axis + x // elems
-                        product = product + mul(jm[k, e], pool[x % elems])
-                    racc[...] += product[LANES:tall]
-                    triple = mul(pt[e], product.astype(jnp.bfloat16))
-                    total = triple if total is None else total + triple
-                acc[...] += total
-
-            below = racc[...]
+            total, below = None, None
+            for m in range(members):
+                code = table_ref[nch, r * members + m]
+                e, code = code % elems, code // elems
+                product = mul(jm[0, e], pool[e])
+                for axis in range(3):
+                    x, code = code % (2 * elems), code // (2 * elems)
+                    k = 1 + 2 * axis + x // elems
+                    product = product + mul(jm[k, e], pool[x % elems])
+                last = product[LANES:tall]
+                below = last if below is None else below + last
+                triple = mul(pt[e], product.astype(jnp.bfloat16))
+                total = triple if total is None else total + triple
             spare = lax.broadcasted_iota(jnp.int32, below.shape, 0) == width - LANES
-            acc[LANES:tall, :] += jnp.where(spare, below, 0.0)
-            emit(r, 0, acc[...])
+            emit(r, 0, total, jnp.where(spare, below, 0.0))
             send_row(r, 0)
 
         def pack_row_tail(r):
@@ -421,16 +416,18 @@
             folded = jnp.where(lane_ids(left.shape) < half, left, right)
             msg[r, tail + half : msg_rows, :] = folded.astype(msg.dtype)
 
-        def side_slots(r, axis):
-            pair = (2 * axis, 2 * axis + 1)
-            for d, total in [(d, side_sum(r, d)) for d in pair]:
+        def side_slots(first, axis):
+            todo = [(first + i, d) for i in range(early) for d in (2 * axis, 2 * axis + 1)]
+            for (r, d), total in [(at, side_sum(*at)) for at in todo]:
                 emit(r, 1 + d, total)
             if axis == 2:
-                pack_row_tail(r)
-            for d in pair:
+                for i in range(early):
+                    pack_row_tail(first + i)
+            for r, d in todo:
                 send_row(r, 1 + d)
             if axis == 2:
-                send_row(r, sides)
+                for i in range(early):
+                    send_row(first + i, sides)
 
         axis_faces = [list(range(4, nch)), [2, 3], [0, 1]]
 
@@ -461,7 +458,7 @@
                 pl.loop(0, 2)(lay_out)
                 take_faces(axis_faces[0])
 
-            pl.loop(first, last)(lambda r: side_slots(r, 0))
+            side_slots(first, 0)
 
             @pl.when(part == 0)
             def _():
@@ -474,7 +471,7 @@
                 def _(axis=axis):
                     take_faces(axis_faces[axis])
 
-                pl.loop(first, last)(lambda r, axis=axis: side_slots(r, axis))
+                side_slots(first, axis)
 
         owner = me_z % stride_z == 0
 
@@ -574,8 +571,6 @@
         pltpu.VMEM((aggs_here, msg_rows, LANES), bf16),
         pltpu.VMEM((aggs_here, (sides + 1) * 8, LANES), f32),
         pltpu.VMEM((aggs_here, tall, LANES), f32),
-        pltpu.VMEM((8, width), f32),
-        pltpu.VMEM((tall, width), f32),
         pltpu.VMEM((out_slots, tail, LANES), bf16),
         pltpu.VMEM((LANES * out_slots, LANES), f32),
         pltpu.SemaphoreType.DMA((4,)),

time: 43.8 us -> 43.6 us (level)
  no operation moved by 1% of the time
where the time goes in v7:
time: 43.6 us; the launch traced here: 43.3 us
  Pallas kernels  42.6 us (98%)
  between operations  0.64 us (1%)
    pallas_call x1, Pallas kernels, fused_kernel(): pl.pallas_call(kernel, in_specs=[pl.BlockSpec(memory_space=pl.ANY)] * 6,...  41.2 us
    pallas_call x1, Pallas kernels, stored(): pl.pallas_call(kernel, in_specs=[pl.BlockSpec(memory_space=pltpu.VMEM)] *...  1.44 us

profile of v7, /device:TPU:0, one launch (start us, length us, event | category | flops | bytes accessed | tf_op | source)
XLA Modules:
  0.0 43.3 jit_solution(16953313655565087573)
XLA Ops:
  0.6 41.2 %shard_map.77 = (bf16[7,135,4,135]{3,2,1,0:T(4,128)(2,1)S(1)}, bf16[4,128,128]{2,1,0:T(8,128)(2,1)S(1)}) custom-call(s32[6,32]{1,0:T(8,128)} %bitcast.8, s32[1,32]{1,0:T(1,128)} %bitcast.9, s32[1,4]{1,0:T(1,128)} %bitcast.10, bf16[135,32,135]{2,1,0:T(8,128)(2,1)} %bitcast.7, bf16[7,135,32,135]{3,2,1,0:T(8,128)(2,1)} %bitcast.6, bf16[32,135]{1,0:T(8,128)(2,1)} %res_in.1), custom_call_target="tpu_custom_call" | custom-call | tf_op jit(solution)/shard_map/pallas_call | solution.py:588
  41.8 1.4 %shard_map.78 = (bf16[7,135,4,135]{3,2,1,0:T(4,128)(2,1)S(1)}, bf16[7,135,4,135]{3,2,1,0:T(4,128)(2,1)}, bf16[4,135]{1,0:T(4,128)(2,1)}) custom-call(bf16[7,135,4,135]{3,2,1,0:T(4,128)(2,1)S(1)} %get-tuple-element.6._, bf16[4,128,128]{2,1,0:T(8,128)(2,1)S(1)} %get-tuple-element.7.tail_ref), custom_call_target="tpu_custom_call", output_to_operand_aliasing={{0}: (0, {})} | custom-call | tf_op jit(solution)/shard_map/pallas_call | solution.py:646

commit v8 on v7

--- a/solution.py
+++ b/solution.py
@@ -332,8 +332,8 @@
         def late(piece):
             return int(piece > 4)
 
-        def row_copy(r, piece):
-            at = pl.ds(pl.multiple_of(piece * LANES, LANES), LANES)
+        def row_copy(r, piece, count):
+            at = pl.ds(piece * LANES, count * LANES)
             slot = slot_of(me_z, r)
             last = piece == sides
             return pltpu.make_async_remote_copy(
@@ -345,8 +345,8 @@
                 device_id_type=MESH,
             )
 
-        def self_copy(r, piece):
-            at = pl.ds(pl.multiple_of(piece * LANES, LANES), LANES)
+        def self_copy(r, piece, count):
+            at = pl.ds(piece * LANES, count * LANES)
             slot = slot_of(me_z, r)
             return pltpu.make_async_copy(
                 msg.at[r, at],
@@ -354,16 +354,16 @@
                 self_sem.at[r % per_owner, late(piece)],
             )
 
-        def send_row(r, piece):
+        def send_row(r, piece, count=1):
             sent = present(piece, me_z)
 
             @pl.when((target_of(r) != me_z) & sent)
             def _():
-                row_copy(r, piece).start()
+                row_copy(r, piece, count).start()
 
             @pl.when((target_of(r) == me_z) & sent)
             def _():
-                self_copy(r, piece).start()
+                self_copy(r, piece, count).start()
 
         def emit(r, s, value, more=0.0):
             msg[r, s * LANES : (s + 1) * LANES, :] = value[:LANES, :LANES].astype(msg.dtype)
@@ -416,18 +416,20 @@
             folded = jnp.where(lane_ids(left.shape) < half, left, right)
             msg[r, tail + half : msg_rows, :] = folded.astype(msg.dtype)
 
-        def side_slots(first, axis):
-            todo = [(first + i, d) for i in range(early) for d in (2 * axis, 2 * axis + 1)]
+        def side_slots(rows, wanted):
+            todo = [(r, d) for r in rows for d in wanted]
             for (r, d), total in [(at, side_sum(*at)) for at in todo]:
                 emit(r, 1 + d, total)
-            if axis == 2:
-                for i in range(early):
-                    pack_row_tail(first + i)
-            for r, d in todo:
-                send_row(r, 1 + d)
-            if axis == 2:
-                for i in range(early):
-                    send_row(first + i, sides)
+            complete = sides - 2 in wanted
+            if complete:
+                for r in rows:
+                    pack_row_tail(r)
+            for r in rows:
+                if not complete:
+                    send_row(r, 1 + wanted[0], len(wanted))
+                    continue
+                for piece in (*(1 + d for d in wanted), sides):
+                    send_row(r, piece)
 
         axis_faces = [list(range(4, nch)), [2, 3], [0, 1]]
 
@@ -449,29 +451,21 @@
                 def _(way=way, step=step):
                     pl.semaphore_wait(relay_sem.at[way, step], 1)
 
-        @pl.loop(0, 2)
-        def _(part):
-            first, last = part * early, part * early + early
-
-            @pl.when(part == 0)
-            def _():
-                pl.loop(0, 2)(lay_out)
-                take_faces(axis_faces[0])
-
-            side_slots(first, 0)
-
-            @pl.when(part == 0)
-            def _():
-                pl.loop(2, sides)(lay_out)
-
-            pl.loop(first, last)(own_slot)
-            for axis in (1, 2):
-
-                @pl.when(part == 0)
-                def _(axis=axis):
-                    take_faces(axis_faces[axis])
-
-                side_slots(first, axis)
+        far_rows = list(range(early))
+        pl.loop(0, 2)(lay_out)
+        take_faces(axis_faces[0])
+        side_slots(far_rows, (0, 1))
+        pl.loop(2, sides)(lay_out)
+        pl.loop(0, early)(own_slot)
+        for axis in (1, 2):
+            take_faces(axis_faces[axis])
+            side_slots(far_rows, (2 * axis, 2 * axis + 1))
+
+        @pl.loop(early, aggs_here)
+        def _(r):
+            own_slot(r)
+            side_slots([r], (0, 1, 2, 3))
+            side_slots([r], (4, 5))
 
         owner = me_z % stride_z == 0
 

time: 43.6 us -> 42.7 us (0.979)
  Pallas kernels: 42.6 us -> 41.8 us
    pallas_call x1, Pallas kernels: 41.2 us -> 40.3 us  [fused_kernel(): pl.pallas_call(kernel, in_specs=[pl.BlockSpec(memory_space=pl.ANY)] * 6,...]
where the time goes in v8:
time: 42.7 us; the launch traced here: 42.4 us
  Pallas kernels  41.8 us (98%)
  between operations  0.64 us (1%)
    pallas_call x1, Pallas kernels, fused_kernel(): pl.pallas_call(kernel, in_specs=[pl.BlockSpec(memory_space=pl.ANY)] * 6,...  40.3 us
    pallas_call x1, Pallas kernels, stored(): pl.pallas_call(kernel, in_specs=[pl.BlockSpec(memory_space=pltpu.VMEM)] *...  1.44 us

profile of v8, /device:TPU:0, one launch (start us, length us, event | category | flops | bytes accessed | tf_op | source)
XLA Modules:
  0.0 42.4 jit_solution(592818566311644999)
XLA Ops:
  0.6 40.3 %shard_map.77 = (bf16[7,135,4,135]{3,2,1,0:T(4,128)(2,1)S(1)}, bf16[4,128,128]{2,1,0:T(8,128)(2,1)S(1)}) custom-call(s32[6,32]{1,0:T(8,128)} %bitcast.8, s32[1,32]{1,0:T(1,128)} %bitcast.9, s32[1,4]{1,0:T(1,128)} %bitcast.10, bf16[135,32,135]{2,1,0:T(8,128)(2,1)} %bitcast.7, bf16[7,135,32,135]{3,2,1,0:T(8,128)(2,1)} %bitcast.6, bf16[32,135]{1,0:T(8,128)(2,1)} %res_in.1), custom_call_target="tpu_custom_call" | custom-call | tf_op jit(solution)/shard_map/pallas_call | solution.py:582
  41.0 1.4 %shard_map.78 = (bf16[7,135,4,135]{3,2,1,0:T(4,128)(2,1)S(1)}, bf16[7,135,4,135]{3,2,1,0:T(4,128)(2,1)}, bf16[4,135]{1,0:T(4,128)(2,1)}) custom-call(bf16[7,135,4,135]{3,2,1,0:T(4,128)(2,1)S(1)} %get-tuple-element.6._, bf16[4,128,128]{2,1,0:T(8,128)(2,1)S(1)} %get-tuple-element.7.tail_ref), custom_call_target="tpu_custom_call", output_to_operand_aliasing={{0}: (0, {})} | custom-call | tf_op jit(solution)/shard_map/pallas_call | solution.py:640

commit v9 on v8

--- a/solution.py
+++ b/solution.py
@@ -189,9 +189,13 @@
             there = me[axis] - step
             return pl.when((there >= 0) & (there < size[axis]))
 
+        def chunk_of(c):
+            return CHUNK if c < 2 else channels[c][2]
+
         def face_parts(c):
             count = channels[c][2]
-            parts = [(n * LANES, CHUNK * LANES) for n in range(0, count, CHUNK)]
+            step = chunk_of(c)
+            parts = [(n * LANES, step * LANES) for n in range(0, count, step)]
             return parts + [(count * LANES, count * 8 + full)]
 
         def face_copy(c, part):
@@ -238,7 +242,7 @@
             for part in range(max(len(face_parts(c)) for c in group)):
                 for c in group:
                     if part < len(face_parts(c)) - 1:
-                        for n in range(part * CHUNK, (part + 1) * CHUNK):
+                        for n in range(part * chunk_of(c), (part + 1) * chunk_of(c)):
                             pack(c, n)
                     elif part < len(face_parts(c)):
                         pack_tail(c)

time: 42.7 us -> 42.7 us (level)
  no operation moved by 1% of the time
where the time goes in v9:
time: 42.7 us; the launch traced here: 42.4 us
  Pallas kernels  41.8 us (98%)
  between operations  0.64 us (1%)
    pallas_call x1, Pallas kernels, fused_kernel(): pl.pallas_call(kernel, in_specs=[pl.BlockSpec(memory_space=pl.ANY)] * 6,...  40.3 us
    pallas_call x1, Pallas kernels, stored(): pl.pallas_call(kernel, in_specs=[pl.BlockSpec(memory_space=pltpu.VMEM)] *...  1.44 us

profile of v9, /device:TPU:0, one launch (start us, length us, event | category | flops | bytes accessed | tf_op | source)
XLA Modules:
  0.0 42.4 jit_solution(15682513817997812935)
XLA Ops:
  0.6 40.3 %shard_map.77 = (bf16[7,135,4,135]{3,2,1,0:T(4,128)(2,1)S(1)}, bf16[4,128,128]{2,1,0:T(8,128)(2,1)S(1)}) custom-call(s32[6,32]{1,0:T(8,128)} %bitcast.8, s32[1,32]{1,0:T(1,128)} %bitcast.9, s32[1,4]{1,0:T(1,128)} %bitcast.10, bf16[135,32,135]{2,1,0:T(8,128)(2,1)} %bitcast.7, bf16[7,135,32,135]{3,2,1,0:T(8,128)(2,1)} %bitcast.6, bf16[32,135]{1,0:T(8,128)(2,1)} %res_in.1), custom_call_target="tpu_custom_call" | custom-call | tf_op jit(solution)/shard_map/pallas_call | solution.py:586
  41.0 1.4 %shard_map.78 = (bf16[7,135,4,135]{3,2,1,0:T(4,128)(2,1)S(1)}, bf16[7,135,4,135]{3,2,1,0:T(4,128)(2,1)}, bf16[4,135]{1,0:T(4,128)(2,1)}) custom-call(bf16[7,135,4,135]{3,2,1,0:T(4,128)(2,1)S(1)} %get-tuple-element.6._, bf16[4,128,128]{2,1,0:T(8,128)(2,1)S(1)} %get-tuple-element.7.tail_ref), custom_call_target="tpu_custom_call", output_to_operand_aliasing={{0}: (0, {})} | custom-call | tf_op jit(solution)/shard_map/pallas_call | solution.py:644
